TPU v7x, 32 devices: a whole 2x2x4 slice. The times are simulated.
32 devices in a mesh: face: 4 (over x, core), tile: 8 (over z, y).
Axes of the slice: x: 2, y: 2, z: 4, core: 2. Of those that a mesh axis runs over, the one named last changes fastest.
Arguments:
- field_in: bfloat16 [12, 48, 256, 256], P('face', None, 'tile'), may hold values from -6 to 6
- out_grad: bfloat16 [12, 48, 256, 256], P('face', None, 'tile'), may hold values from -6 to 6
- weight_first: bfloat16 [48, 48, 3, 3], replicated, may hold values from -0.3125 to 0.3125
- bias_first: float32 [48], replicated, may hold values from -3 to 3
- weight_second: bfloat16 [48, 48, 3, 3], replicated, may hold values from -0.3125 to 0.3125
- bias_second: float32 [48], replicated, may hold values from -3 to 3
- face_links: int32 [12, 4, 3], replicated, may hold values from 0 to 11, as said below
- corner_rules: int32 [12, 4], replicated, may hold values from 0 to 1
Outputs:
- output_field: bfloat16 [12, 48, 256, 256], P('face', None, 'tile')
- grad_field: bfloat16 [12, 48, 256, 256], P('face', None, 'tile')
- grad_weight_first: float32 [48, 48, 3, 3], replicated
- grad_bias_first: float32 [48], replicated
- grad_weight_second: float32 [48, 48, 3, 3], replicated
- grad_bias_second: float32 [48], replicated
Inputs may be any that keep to these rules, and one draw needn't show every extreme that they name: face_links[f, e] = (g, e2, r) glues edge e of face f to edge e2 of face g; r = 1 when positions along the two edges run in opposite directions. The gluing is a pairing: (g, e2) differs from (f, e) and face_links[g, e2] = (f, e, r). The partner face lies in 0..11, the edge in 0..3, the flag in 0..1.
All inputs are finite; a program needn't handle non-finite values.
Results may differ from a plain program's by a relative error of at most 0.0055.
The roundings to bfloat16 on the way count: a program that leaves them out, or rounds other values in their place, can miss the bound.
Values may be sent and summed in bfloat16 or wider, within the bound.
A program may use at most 256 MiB of HBM per device.

v0:
```python
import jax
import jax.numpy as jnp
from jax import lax
from jax.sharding import PartitionSpec as P

INV_ROOT_TWO = 0.7071067811865476
INV_ROOT_TWO_PI = 0.3989422804014327


def shortened(x):
    return jax.tree.map(lambda a: a.astype(jnp.bfloat16) if a.dtype == jnp.float32 else a, x)


def extended_2(block, sides, width):
    for axis, dim in sides:
        count = lax.axis_size(axis)
        forward = [(i, i + 1) for i in range(count - 1)]
        backward = [(target, source) for source, target in forward]
        low = lax.ppermute(
            lax.slice_in_dim(block, block.shape[dim] - width, None, axis=dim), axis, forward
        )
        high = lax.ppermute(lax.slice_in_dim(block, 0, width, axis=dim), axis, backward)
        block = jnp.concatenate([low, block, high], axis=dim)
    return block


def gelu_pair(values):
    normal_cdf = 0.5 * (1.0 + lax.erf(values * INV_ROOT_TWO))
    normal_pdf = jnp.exp(-0.5 * values * values) * INV_ROOT_TWO_PI
    return (values * normal_cdf, normal_cdf + values * normal_pdf)


def convolve(padded, weight):
    return lax.conv_general_dilated(
        padded,
        weight,
        (1, 1),
        "VALID",
        dimension_numbers=("NCHW", "OIHW", "NCHW"),
        preferred_element_type=jnp.float32,
    )


def halo_rows(strip):
    return extended_2(shortened(strip), (("tile", 2),), 1).astype(strip.dtype)


def place_lines(north_row, south_row, west_part, east_part, tile_pos, tile_count):
    seg_len = west_part.shape[-1]
    mirrored = tile_count - 1 - tile_pos
    blanks = jnp.zeros(north_row.shape, jnp.float32)
    north_full = jnp.where(tile_pos == 0, north_row.astype(jnp.float32), blanks)
    south_full = jnp.where(tile_pos == tile_count - 1, south_row.astype(jnp.float32), blanks)
    west_wide = west_part.astype(jnp.float32)
    east_wide = east_part.astype(jnp.float32)
    west_full = lax.dynamic_update_slice_in_dim(blanks, west_wide, tile_pos * seg_len, 2)
    east_full = lax.dynamic_update_slice_in_dim(blanks, east_wide, tile_pos * seg_len, 2)
    placed = jnp.stack([north_full, south_full, west_full, east_full], axis=1)
    own_lines = lax.psum(placed.astype(jnp.bfloat16), "tile")
    front = lax.dynamic_slice_in_dim(own_lines, tile_pos * seg_len, seg_len, 3)
    back = lax.dynamic_slice_in_dim(own_lines, mirrored * seg_len, seg_len, 3)
    return (front, back)


def partner_pieces(front, my_links, tile_pos, tile_count):
    faces_dev, _, channels, seg_len = front.shape
    side_len = seg_len * tile_count
    partner_face = my_links[:, :, 0].reshape(-1)
    partner_edge = my_links[:, :, 1].reshape(-1)
    flip_mask = (my_links[:, :, 2] == 1).reshape(-1)
    gathered = lax.all_gather(front, ("face", "tile"), axis=3, tiled=True)

    def fetch_line(face_id, edge_id):
        start = (face_id % faces_dev, edge_id, 0, face_id // faces_dev * side_len)
        return lax.dynamic_slice(gathered, start, (1, 1, channels, side_len))[0, 0]

    source = jax.vmap(fetch_line)(partner_face, partner_edge)
    ghosts = jnp.where(flip_mask[:, None, None], source[:, :, ::-1], source)
    ghosts = ghosts.reshape(faces_dev, 4, channels, side_len)
    north_row = ghosts[:, 0]
    south_row = ghosts[:, 1]
    west_part = lax.dynamic_slice_in_dim(ghosts[:, 2], tile_pos * seg_len, seg_len, 2)
    east_part = lax.dynamic_slice_in_dim(ghosts[:, 3], tile_pos * seg_len, seg_len, 2)
    return (north_row, south_row, west_part, east_part)


def fill_strip(activation, my_links, my_corners, tile_pos, tile_count):
    front, back = place_lines(
        activation[:, :, 0, :],
        activation[:, :, -1, :],
        activation[:, :, :, 0],
        activation[:, :, :, -1],
        tile_pos,
        tile_count,
    )
    north_row, south_row, west_part, east_part = partner_pieces(
        front, my_links, tile_pos, tile_count
    )
    corner_code = (my_corners == 0)[:, :, None]
    corner_nw = jnp.where(corner_code[:, 0], north_row[:, :, 0], west_part[:, :, 0])
    corner_ne = jnp.where(corner_code[:, 1], north_row[:, :, -1], east_part[:, :, 0])
    corner_sw = jnp.where(corner_code[:, 2], south_row[:, :, 0], west_part[:, :, -1])
    corner_se = jnp.where(corner_code[:, 3], south_row[:, :, -1], east_part[:, :, -1])
    middle = jnp.concatenate(
        [west_part[:, :, :, None], activation, east_part[:, :, :, None]], axis=3
    )
    extended = halo_rows(middle)
    top_row = jnp.concatenate([corner_nw[:, :, None], north_row, corner_ne[:, :, None]], axis=2)
    bottom_row = jnp.concatenate([corner_sw[:, :, None], south_row, corner_se[:, :, None]], axis=2)
    top_rim = jnp.where(tile_pos == 0, top_row, extended[:, :, 0])
    bottom_rim = jnp.where(tile_pos == tile_count - 1, bottom_row, extended[:, :, -1])
    return jnp.concatenate(
        [top_rim[:, :, None], extended[:, :, 1:-1], bottom_rim[:, :, None]], axis=2
    )


def unfold_strip(cotangent, weight, my_links, my_corners, tile_pos, tile_count):
    widened = jnp.pad(cotangent, ((0, 0), (0, 0), (0, 0), (1, 1)))
    extended = halo_rows(widened)
    padded = jnp.pad(extended, ((0, 0), (0, 0), (1, 1), (1, 1)))
    flipped = jnp.transpose(weight[:, :, ::-1, ::-1], (1, 0, 2, 3))
    pad_grad = convolve(padded, flipped)
    at_top = tile_pos == 0
    at_bottom = tile_pos == tile_count - 1
    north_row = pad_grad[:, :, 0, 1:-1]
    south_row = pad_grad[:, :, -1, 1:-1]
    west_part = pad_grad[:, :, 1:-1, 0]
    east_part = pad_grad[:, :, 1:-1, -1]
    corner_nw = pad_grad[:, :, 0, 0]
    corner_ne = pad_grad[:, :, 0, -1]
    corner_sw = pad_grad[:, :, -1, 0]
    corner_se = pad_grad[:, :, -1, -1]
    corner_code = my_corners[:, :, None]
    north_row = north_row.at[:, :, 0].add(jnp.where(corner_code[:, 0] == 0, corner_nw, 0.0))
    north_row = north_row.at[:, :, -1].add(jnp.where(corner_code[:, 1] == 0, corner_ne, 0.0))
    south_row = south_row.at[:, :, 0].add(jnp.where(corner_code[:, 2] == 0, corner_sw, 0.0))
    south_row = south_row.at[:, :, -1].add(jnp.where(corner_code[:, 3] == 0, corner_se, 0.0))
    west_part = west_part.at[:, :, 0].add(
        jnp.where((corner_code[:, 0] == 1) & at_top, corner_nw, 0.0)
    )
    west_part = west_part.at[:, :, -1].add(
        jnp.where((corner_code[:, 2] == 1) & at_bottom, corner_sw, 0.0)
    )
    east_part = east_part.at[:, :, 0].add(
        jnp.where((corner_code[:, 1] == 1) & at_top, corner_ne, 0.0)
    )
    east_part = east_part.at[:, :, -1].add(
        jnp.where((corner_code[:, 3] == 1) & at_bottom, corner_se, 0.0)
    )
    front, back = place_lines(
        north_row.astype(jnp.bfloat16),
        south_row.astype(jnp.bfloat16),
        west_part.astype(jnp.bfloat16),
        east_part.astype(jnp.bfloat16),
        tile_pos,
        tile_count,
    )
    back_north, back_south, back_west, back_east = partner_pieces(
        front, my_links, tile_pos, tile_count
    )
    interior = pad_grad[:, :, 1:-1, 1:-1]
    interior = interior.at[:, :, 0, :].add(jnp.where(at_top, back_north.astype(jnp.float32), 0.0))
    interior = interior.at[:, :, -1, :].add(
        jnp.where(at_bottom, back_south.astype(jnp.float32), 0.0)
    )
    interior = interior.at[:, :, :, 0].add(back_west.astype(jnp.float32))
    interior = interior.at[:, :, :, -1].add(back_east.astype(jnp.float32))
    return interior


def weight_grad(cotangent, padded):
    return lax.conv_general_dilated(
        padded,
        cotangent,
        (1, 1),
        "VALID",
        dimension_numbers=("CNHW", "IOHW", "CNHW"),
        preferred_element_type=jnp.float32,
    )


def body(
    field_in,
    out_grad,
    weight_first,
    bias_first,
    weight_second,
    bias_second,
    face_links,
    corner_rules,
):
    tile_count = lax.axis_size("tile")
    tile_pos = lax.axis_index("tile")
    face_pos = lax.axis_index("face")
    faces_dev = field_in.shape[0]
    side_len = field_in.shape[3]
    my_links = lax.dynamic_slice_in_dim(face_links, face_pos * faces_dev, faces_dev, 0)
    my_corners = lax.dynamic_slice_in_dim(corner_rules, face_pos * faces_dev, faces_dev, 0)
    padded_first = fill_strip(field_in, my_links, my_corners, tile_pos, tile_count)
    pre_first = convolve(padded_first, weight_first) + bias_first[None, :, None, None]
    gelu_first, slope_first = gelu_pair(pre_first)
    hidden = gelu_first.astype(jnp.bfloat16)
    padded_second = fill_strip(hidden, my_links, my_corners, tile_pos, tile_count)
    pre_second = convolve(padded_second, weight_second) + bias_second[None, :, None, None]
    gelu_second, slope_second = gelu_pair(pre_second)
    output_field = gelu_second.astype(jnp.bfloat16)
    grad_second = (out_grad.astype(jnp.float32) * slope_second).astype(jnp.bfloat16)
    weight_second_part = weight_grad(grad_second, padded_second)
    bias_second_part = jnp.sum(grad_second.astype(jnp.float32), axis=(0, 2, 3))
    grad_hidden = unfold_strip(
        grad_second, weight_second, my_links, my_corners, tile_pos, tile_count
    )
    grad_first = (grad_hidden * slope_first).astype(jnp.bfloat16)
    weight_first_part = weight_grad(grad_first, padded_first)
    bias_first_part = jnp.sum(grad_first.astype(jnp.float32), axis=(0, 2, 3))
    grad_field = unfold_strip(
        grad_first, weight_first, my_links, my_corners, tile_pos, tile_count
    ).astype(jnp.bfloat16)
    totals = lax.psum(
        (weight_first_part, bias_first_part, weight_second_part, bias_second_part), ("face", "tile")
    )
    return (
        output_field,
        grad_field,
        totals[0] / side_len,
        totals[1] / side_len,
        totals[2] / side_len,
        totals[3] / side_len,
    )


def solution(mesh):
    return jax.shard_map(
        body,
        mesh=mesh,
        in_specs=(
            P("face", None, "tile", None),
            P("face", None, "tile", None),
            P(),
            P(),
            P(),
            P(),
            P(),
            P(),
        ),
        out_specs=(
            P("face", None, "tile", None),
            P("face", None, "tile", None),
            P(),
            P(),
            P(),
            P(),
        ),
        check_vma=False,
    )
```

profile of v0, /device:TPU:0, one launch (start us, length us, event | category | flops | bytes accessed | tf_op | source)
XLA Modules:
  0.0 1963.5 jit_solution(1567796698921269111)
XLA Ops:
  19.2 74.5 %all-reduce.10.cloned.1.call-done = bf16[3,4,48,256]{3,2,0,1:T(8,128)(2,1)} async-done(((bf16[3,4,48,256]{3,2,0,1:T(8,128)(2,1)}), bf16[3,4,48,256]{3,2,0,1:T(8,128)(2,1)}) %all-reduce.10.cloned.1.call-update) | async-done | bytes 294928 | tf_op jit(solution)/shard_map/psum | solution.py:59
  103.9 51.9 %all-gather.5.cloned.1.call-done = bf16[3,4,48,1024]{2,1,0,3:T(4,128)(2,1)} async-done(((bf16[3,4,48,32]{2,1,0,3:T(4,128)(2,1)}), bf16[3,4,48,1024]{2,1,0,3:T(4,128)(2,1)}) %all-gather.5.cloned.1.call-update) | async-done | bytes 1179664 | tf_op jit(solution)/shard_map/all_gather | solution.py:71
  179.4 17.8 fusion.87
  203.8 24.2 %copy.2867 = bf16[48,34,3,8,33]{4,3,0,2,1:T(8,128)(2,1)} copy(bf16[48,34,3,8,33]{0,2,4,3,1:T(4,128)(2,1)} %bitcast.324) | data formatting | bytes 5170176 | tf_op jit(solution)/shard_map/conv_general_dilated | solution.py:34
  268.7 23.4 %fusion.8 = (f32[32,24,33,48]{3,1,2,0:T(8,128)}, bf16[32,24,33,48]{3,1,2,0:T(8,128)(2,1)S(1)}) fusion(f32[48]{0:T(128)S(1)} %copy-done.49, pred[24,33]{0,1:T(8,128)(4,1)S(1)} %copy-done.53, bf16[48,48,3,3]{1,0,3,2:T(8,128)(2,1)S(1)} %copy-done.47, bf16[48,34,3,8,35]{0,3,2,4,1:T(8,128)(2,1)} %copy.2762), kind=kOutput, calls=%fused_computation.21 | convolution fusion | flops 1065664512 | bytes 10083288 | tf_op jit(solution)/shard_map/conv_general_dilated | solution.py:34
  311.6 72.2 %all-reduce.12.cloned.1.call-done = bf16[3,4,48,256]{3,2,0,1:T(8,128)(2,1)} async-done(((bf16[3,4,48,256]{3,2,0,1:T(8,128)(2,1)}), bf16[3,4,48,256]{3,2,0,1:T(8,128)(2,1)}) %all-reduce.12.cloned.1.call-update) | async-done | bytes 294928 | tf_op jit(solution)/shard_map/psum | solution.py:59
  386.1 59.4 %all-gather.7.cloned.1.call-done = bf16[3,4,48,1024]{2,1,0,3:T(4,128)(2,1)} async-done(((bf16[3,4,48,32]{2,1,0,3:T(4,128)(2,1)}), bf16[3,4,48,1024]{2,1,0,3:T(4,128)(2,1)}) %all-gather.7.cloned.1.call-update) | async-done | bytes 1179664 | tf_op jit(solution)/shard_map/all_gather | solution.py:71
  468.7 19.1 fusion.84
  494.5 24.2 %copy.2872 = bf16[48,34,3,8,33]{4,3,0,2,1:T(8,128)(2,1)} copy(bf16[48,34,3,8,33]{0,2,4,3,1:T(4,128)(2,1)} %bitcast.325) | data formatting | bytes 5170176 | tf_op jit(solution)/shard_map/conv_general_dilated | solution.py:34
  559.3 22.5 %fusion.12 = (f32[32,24,33,48]{3,1,2,0:T(8,128)}, bf16[32,24,33,48]{3,1,2,0:T(8,128)(2,1)}) fusion(f32[48]{0:T(128)S(1)} %copy-done.50, pred[24,33]{0,1:T(8,128)(4,1)S(1)} %copy-done.53, bf16[48,48,3,3]{1,0,3,2:T(8,128)(2,1)S(1)} %copy-done, bf16[48,34,3,8,35]{0,3,2,4,1:T(8,128)(2,1)} %copy.2782), kind=kOutput, calls=%fused_computation.25 | convolution fusion | flops 1065664512 | bytes 10083288 | tf_op jit(solution)/shard_map/conv_general_dilated | solution.py:34
  695.0 22.0 %convolution_select_fusion.1 = f32[34,24,33,48]{3,1,2,0:T(8,128)} fusion(bf16[48,48,3,3]{1,0,3,2:T(8,128)(2,1)S(1)} %copy-done, bf16[48,34,3,8,35]{0,3,2,4,1:T(8,128)(2,1)} %copy.2790, pred[24,33]{0,1:T(8,128)(4,1)S(1)} %copy-done.51), kind=kOutput, calls=%fused_computation.37 | convolution fusion | flops 1096153344 | bytes 7954200 | tf_op jit(solution)/shard_map/conv_general_dilated | solution.py:34
  746.3 17.6 copy.2888
  763.9 29.2 %fusion.67 = (f32[3,48,1,256]{2,1,0,3:T(8,128)}, f32[3,48,1,256]{2,1,0,3:T(8,128)}) fusion(f32[3,48,34,258]{2,1,0,3:T(8,128)} %bitcast.309), kind=kLoop, calls=%fused_computation.219 | loop fusion | bytes 589824 | tf_op jit(solution)/shard_map/slice | solution.py:125
  827.7 73.4 %all-reduce.14.cloned.1.call-done = bf16[3,4,48,256]{3,2,0,1:T(8,128)(2,1)} async-done(((bf16[3,4,48,256]{3,2,0,1:T(8,128)(2,1)}), bf16[3,4,48,256]{3,2,0,1:T(8,128)(2,1)}) %all-reduce.14.cloned.1.call-update) | async-done | bytes 294928 | tf_op jit(solution)/shard_map/psum | solution.py:59
  982.5 20.5 %slice_add_fusion.3 = f32[3,48,1,256]{2,1,0,3:T(8,128)} fusion(f32[3,48,1,256]{2,1,0,3:T(8,128)} %copy.2815, f32[3,48,34,258]{2,1,0,3:T(8,128)} %bitcast.315), kind=kLoop, calls=%fused_computation.14 | loop fusion | flops 36864 | bytes 442368 | tf_op jit(solution)/shard_map/add | solution.py:162
  1015.2 43.6 %scatter-add.94 = f32[3,48,32,256]{2,1,0,3:T(8,128)} dynamic-update-slice(f32[3,48,32,256]{2,1,0,3:T(8,128)} %slice.1002, f32[3,48,1,256]{2,1,0,3:T(8,128)} %slice_add_fusion.3, s32[]{:T(128)} %constant.616.clone.1, s32[]{:T(128)} %constant.616.clone.1, s32[]{:T(128)} %constant.616.clone.1, s32[]{:T(128)} %constant.616.clone.1) | dynamic-update-slice | bytes 294916 | tf_op jit(solution)/shard_map/scatter-add | solution.py:162
  1058.8 20.5 %slice_add_fusion.2 = f32[3,48,1,256]{2,1,0,3:T(8,128)} fusion(f32[3,48,1,256]{2,1,0,3:T(8,128)} %copy.2817, f32[3,48,32,256]{2,1,0,3:T(8,128)} %scatter-add.94), kind=kLoop, calls=%fused_computation.13 | loop fusion | flops 36864 | bytes 442368 | tf_op jit(solution)/shard_map/add | solution.py:163
  1079.3 73.5 %scatter-add.95 = f32[3,48,32,256]{2,1,0,3:T(8,128)} dynamic-update-slice(f32[3,48,32,256]{2,1,0,3:T(8,128)} %scatter-add.94, f32[3,48,1,256]{2,1,0,3:T(8,128)} %slice_add_fusion.2, s32[]{:T(128)} %constant.616.clone.1, s32[]{:T(128)} %constant.616.clone.1, s32[]{:T(128)} %constant.635.clone.1, s32[]{:T(128)} %constant.616.clone.1) | dynamic-update-slice | bytes 294916 | tf_op jit(solution)/shard_map/scatter-add | solution.py:163
  1207.5 44.8 %fusion.75 = f32[48,48,3,3]{0,1,3,2:T(8,128)} fusion(bf16[3,48,32,256]{1,0,3,2:T(4,128)(2,1)} %copy.2858, bf16[3,48,1,258]{1,0,3,2:T(4,128)(2,1)S(1)} %copy-done.15, bf16[3,48,32,1]{1,0,3,2:T(4,128)(2,1)S(1)} %copy-done.23, bf16[3,48,32,256]{1,0,3,2:T(4,128)(2,1)} %bitcast.319, bf16[3,48,32,1]{1,0,3,2:T(4,128)(2,1)S(1)} %copy-done.21, ...), kind=kOutput, calls=%fused_computation.227 | convolution fusion | flops 1031847552 | bytes 4968576 | tf_op jit(solution)/shard_map/conv_general_dilated | solution.py:172
  1342.4 21.8 %convolution_select_fusion = f32[34,24,33,48]{3,1,2,0:T(8,128)} fusion(bf16[48,48,3,3]{1,0,3,2:T(8,128)(2,1)S(1)} %copy-done.48, bf16[48,34,3,8,35]{0,3,2,4,1:T(8,128)(2,1)} %copy.2828, pred[24,33]{0,1:T(8,128)(4,1)S(1)} %copy-done.52), kind=kOutput, calls=%fused_computation.36 | convolution fusion | flops 1096153344 | bytes 7954200 | tf_op jit(solution)/shard_map/conv_general_dilated | solution.py:34
  1393.4 17.6 copy.2892
  1411.1 29.3 %fusion.66 = (f32[3,48,1,256]{2,1,0,3:T(8,128)}, f32[3,48,1,256]{2,1,0,3:T(8,128)}) fusion(f32[3,48,34,258]{2,1,0,3:T(8,128)} %bitcast.302), kind=kLoop, calls=%fused_computation.218 | loop fusion | bytes 589824 | tf_op jit(solution)/shard_map/slice | solution.py:125
  1475.1 44.8 %fusion.74 = f32[48,48,3,3]{0,1,3,2:T(8,128)} fusion(bf16[3,48,32,256]{1,0,3,2:T(4,128)(2,1)} %copy.2857, bf16[3,48,1,258]{1,0,3,2:T(4,128)(2,1)S(1)} %copy-done.11, bf16[3,48,32,1]{1,0,3,2:T(4,128)(2,1)S(1)} %copy-done.19, bf16[3,48,32,256]{1,0,3,2:T(4,128)(2,1)} %copy.2758, bf16[3,48,32,1]{1,0,3,2:T(4,128)(2,1)S(1)} %copy-done.17, ...), kind=kOutput, calls=%fused_computation.226 | convolution fusion | flops 1031847552 | bytes 4968576 | tf_op jit(solution)/shard_map/conv_general_dilated | solution.py:172
  1520.2 28.0 %all-reduce.16.cloned.1.call-done = bf16[3,4,48,256]{3,2,0,1:T(8,128)(2,1)} async-done(((bf16[3,4,48,256]{3,2,0,1:T(8,128)(2,1)}), bf16[3,4,48,256]{3,2,0,1:T(8,128)(2,1)}) %all-reduce.16.cloned.1.call-update) | async-done | bytes 294928 | tf_op jit(solution)/shard_map/psum | solution.py:59
  1567.9 39.3 %all-reduce.2 = (f32[48]{0:T(128)S(1)}, f32[48]{0:T(128)S(1)}) all-reduce(f32[48]{0:T(128)S(1)} %copy-done.46, f32[48]{0:T(128)S(1)} %copy-done.45), channel_id=1, replica_groups=mesh['face'=4,'tile'=8] {'face','tile'}, use_global_device_ids=true, to_apply=%region_6.7 | all-reduce | flops 96 | bytes 768 | tf_op jit(solution)/shard_map/psum | solution.py:219
  1608.3 16.6 slice.1030
  1624.9 54.6 %all-reduce.18.cloned.1.call-done = (f32[48,48,3,3]{0,1,3,2:T(8,128)}, f32[48,48,3,3]{0,1,3,2:T(8,128)}) async-done(((f32[48,48,3,3]{0,1,3,2:T(8,128)}, f32[48,48,3,3]{0,1,3,2:T(8,128)}), (f32[48,48,3,3]{0,1,3,2:T(8,128)}, f32[48,48,3,3]{0,1,3,2:T(8,128)})) %all-reduce.18.cloned.1.call-update) | async-done | bytes 165904 | tf_op jit(solution)/shard_map/psum | solution.py:219
  1683.1 60.5 %all-gather.11.cloned.1.call-done = bf16[3,4,48,1024]{2,1,0,3:T(4,128)(2,1)} async-done(((bf16[3,4,48,32]{2,1,0,3:T(4,128)(2,1)}), bf16[3,4,48,1024]{2,1,0,3:T(4,128)(2,1)}) %all-gather.11.cloned.1.call-update) | async-done | bytes 1179664 | tf_op jit(solution)/shard_map/all_gather | solution.py:71
  1760.6 20.5 %slice_add_fusion.1 = f32[3,48,1,256]{2,1,0,3:T(8,128)} fusion(f32[3,48,1,256]{2,1,0,3:T(8,128)} %copy.2852, f32[3,48,34,258]{2,1,0,3:T(8,128)} %bitcast.308), kind=kLoop, calls=%fused_computation.12 | loop fusion | flops 36864 | bytes 442368 | tf_op jit(solution)/shard_map/add | solution.py:162
  1793.3 43.6 %scatter-add.114 = f32[3,48,32,256]{2,1,0,3:T(8,128)} dynamic-update-slice(f32[3,48,32,256]{2,1,0,3:T(8,128)} %slice.1030, f32[3,48,1,256]{2,1,0,3:T(8,128)} %slice_add_fusion.1, s32[]{:T(128)} %constant.616.clone.1, s32[]{:T(128)} %constant.616.clone.1, s32[]{:T(128)} %constant.616.clone.1, s32[]{:T(128)} %constant.616.clone.1) | dynamic-update-slice | bytes 294916 | tf_op jit(solution)/shard_map/scatter-add | solution.py:162
  1836.9 20.5 %slice_add_fusion = f32[3,48,1,256]{2,1,0,3:T(8,128)} fusion(f32[3,48,1,256]{2,1,0,3:T(8,128)} %copy.2854, f32[3,48,32,256]{2,1,0,3:T(8,128)} %scatter-add.114), kind=kLoop, calls=%fused_computation.11 | loop fusion | flops 36864 | bytes 442368 | tf_op jit(solution)/shard_map/add | solution.py:163
  1857.4 73.6 %scatter-add.115 = f32[3,48,32,256]{2,1,0,3:T(8,128)} dynamic-update-slice(f32[3,48,32,256]{2,1,0,3:T(8,128)} %scatter-add.114, f32[3,48,1,256]{2,1,0,3:T(8,128)} %slice_add_fusion, s32[]{:T(128)} %constant.616.clone.1, s32[]{:T(128)} %constant.616.clone.1, s32[]{:T(128)} %constant.635.clone.1, s32[]{:T(128)} %constant.616.clone.1) | dynamic-update-slice | bytes 294916 | tf_op jit(solution)/shard_map/scatter-add | solution.py:163
  (365 shorter events, 742.8 us)
Async XLA Ops:
  7.2 552.1 %copy-start = (bf16[48,48,3,3]{1,0,3,2:T(8,128)(2,1)S(1)}, bf16[48,48,3,3]{1,0,3,2:T(8,128)(2,1)}, u32[]{:S(2)}) copy-start(bf16[48,48,3,3]{1,0,3,2:T(8,128)(2,1)} %param.60) | copy-start | bytes 124420
  7.2 86.5 %all-reduce.10.cloned.1.call-start = ((), (), s32[]{:S(2)}) async-start(), calls=%async_computation | async-start | bytes 589824 | tf_op jit(solution)/shard_map/psum | solution.py:59
  7.2 95.1 %copy-start.24 = (s32[12,4,3]{0,1,2:T(4,128)S(1)}, s32[12,4,3]{0,1,2:T(4,128)}, u32[]{:S(2)}) copy-start(s32[12,4,3]{0,1,2:T(4,128)} %param.62) | copy-start | bytes 1732
  7.3 96.2 %copy-start.44 = (s32[12,4]{0,1:T(4,128)S(1)}, s32[12,4]{0,1:T(4,128)}, u32[]{:S(2)}) copy-start(s32[12,4]{0,1:T(4,128)} %param.63) | copy-start | bytes 580
  19.2 136.6 %all-gather.5.cloned.1.call-start = ((), (), s32[]{:S(2)}) async-start(), calls=%async_computation.1 | async-start | bytes 3244032 | tf_op jit(solution)/shard_map/all_gather | solution.py:71
  95.5 288.4 %all-reduce.12.cloned.1.call-start = ((), (), s32[]{:S(2)}) async-start(), calls=%async_computation.2 | async-start | bytes 589824 | tf_op jit(solution)/shard_map/psum | solution.py:59
  103.4 345.8 %copy-start.25 = (pred[12]{0:T(512)(128)(4,1)}, pred[12]{0:T(512)(128)(4,1)S(1)}, u32[]{:S(2)}) copy-start(pred[12]{0:T(512)(128)(4,1)S(1)} %eq.133) | copy-start | bytes 40
  103.9 341.6 %copy-start.5 = (s32[12]{0:T(128)}, s32[12]{0:T(128)S(1)}, u32[]{:S(2)}) copy-start(s32[12]{0:T(128)S(1)} %fusion.63) | copy-start | bytes 148
  163.5 15.4 collective-permute-start
  167.1 12.0 collective-permute-start.1
  311.6 133.8 %all-gather.7.cloned.1.call-start = ((), (), s32[]{:S(2)}) async-start(), calls=%async_computation.3 | async-start | bytes 3244032 | tf_op jit(solution)/shard_map/all_gather | solution.py:71
  385.7 515.3 %all-reduce.14.cloned.1.call-start = ((), (), s32[]{:S(2)}) async-start(), calls=%async_computation.4 | async-start | bytes 589824 | tf_op jit(solution)/shard_map/psum | solution.py:59
  453.0 15.2 collective-permute-start.2
  456.4 12.0 collective-permute-start.3
  621.6 13.5 collective-permute-start.4
  626.0 9.2 collective-permute-start.5
  627.6 192.9 %copy-start.38 = (pred[3]{0:T(512)(128)(4,1)}, pred[3]{0:T(512)(128)(4,1)S(1)}, u32[]{:S(2)}) copy-start(pred[3]{0:T(512)(128)(4,1)S(1)} %get-tuple-element.458) | copy-start | bytes 13
  627.6 192.9 %copy-start.40 = (pred[3]{0:T(512)(128)(4,1)}, pred[3]{0:T(512)(128)(4,1)S(1)}, u32[]{:S(2)}) copy-start(pred[3]{0:T(512)(128)(4,1)S(1)} %get-tuple-element.462) | copy-start | bytes 13
  627.6 192.9 %copy-start.42 = (pred[3]{0:T(512)(128)(4,1)}, pred[3]{0:T(512)(128)(4,1)S(1)}, u32[]{:S(2)}) copy-start(pred[3]{0:T(512)(128)(4,1)S(1)} %get-tuple-element.463) | copy-start | bytes 13
  627.6 194.6 %copy-start.30 = (pred[3]{0:T(512)(128)(4,1)}, pred[3]{0:T(512)(128)(4,1)S(1)}, u32[]{:S(2)}) copy-start(pred[3]{0:T(512)(128)(4,1)S(1)} %get-tuple-element.456) | copy-start | bytes 13
  627.6 194.6 %copy-start.32 = (pred[3]{0:T(512)(128)(4,1)}, pred[3]{0:T(512)(128)(4,1)S(1)}, u32[]{:S(2)}) copy-start(pred[3]{0:T(512)(128)(4,1)S(1)} %get-tuple-element.457) | copy-start | bytes 13
  627.6 194.6 %copy-start.34 = (pred[3]{0:T(512)(128)(4,1)}, pred[3]{0:T(512)(128)(4,1)S(1)}, u32[]{:S(2)}) copy-start(pred[3]{0:T(512)(128)(4,1)S(1)} %get-tuple-element.460) | copy-start | bytes 13
  627.6 194.6 %copy-start.36 = (pred[3]{0:T(512)(128)(4,1)}, pred[3]{0:T(512)(128)(4,1)S(1)}, u32[]{:S(2)}) copy-start(pred[3]{0:T(512)(128)(4,1)S(1)} %get-tuple-element.461) | copy-start | bytes 13
  627.6 196.8 %copy-start.28 = (pred[3]{0:T(512)(128)(4,1)}, pred[3]{0:T(512)(128)(4,1)S(1)}, u32[]{:S(2)}) copy-start(pred[3]{0:T(512)(128)(4,1)S(1)} %get-tuple-element.459) | copy-start | bytes 13
  827.6 137.4 %all-gather.9.cloned.1.call-start = ((), (), s32[]{:S(2)}) async-start(), calls=%async_computation.5 | async-start | bytes 3244032 | tf_op jit(solution)/shard_map/all_gather | solution.py:71
  902.8 645.3 %all-reduce.16.cloned.1.call-start = ((), (), s32[]{:S(2)}) async-start(), calls=%async_computation.6 | async-start | bytes 589824 | tf_op jit(solution)/shard_map/psum | solution.py:59
  1191.2 90.2 %collective-permute-start.6 = (bf16[3,48,1,258]{3,1,2,0:T(8,128)(2,1)}, bf16[3,48,1,258]{3,1,2,0:T(8,128)(2,1)}, u32[]{:S(2)}, u32[]{:S(2)}) collective-permute-start(bf16[3,48,1,258]{3,1,2,0:T(8,128)(2,1)} %copy.2824), channel_id=1, source_target_pairs={{0,1},{1,2},{2,3},{3,4},{4,5},{5,6},{6,7},{8,9},{9,10},{10,11},{11... | collective-permute-start | bytes 222920 | tf_op jit(solution)/shard_map/ppermute | solution.py:19
  1206.2 75.3 %collective-permute-start.7 = (bf16[3,48,1,258]{3,1,2,0:T(8,128)(2,1)}, bf16[3,48,1,258]{3,1,2,0:T(8,128)(2,1)}, u32[]{:S(2)}, u32[]{:S(2)}) collective-permute-start(bf16[3,48,1,258]{3,1,2,0:T(8,128)(2,1)} %copy.2825), channel_id=1, source_target_pairs={{1,0},{2,1},{3,2},{4,3},{5,4},{6,5},{7,6},{9,8},{10,9},{11,10},{12... | collective-permute-start | bytes 222920 | tf_op jit(solution)/shard_map/ppermute | solution.py:22
  1475.0 204.6 %all-reduce.18.cloned.1.call-start = ((), (), s32[]{:S(2)}) async-start(), calls=%async_computation.8 | async-start | bytes 884736 | tf_op jit(solution)/shard_map/psum | solution.py:219
  1519.9 223.6 %all-gather.11.cloned.1.call-start = ((), (), s32[]{:S(2)}) async-start(), calls=%async_computation.7 | async-start | bytes 3244032 | tf_op jit(solution)/shard_map/all_gather | solution.py:71
  1608.3 135.2 %copy-start.7 = (s32[12]{0:T(128)S(1)}, s32[12]{0:T(128)}, u32[]{:S(2)}) copy-start(s32[12]{0:T(128)} %copy-done.5) | copy-start | bytes 148
  1608.3 139.0 %copy-start.27 = (pred[12]{0:T(512)(128)(4,1)S(1)}, pred[12]{0:T(512)(128)(4,1)}, u32[]{:S(2)}) copy-start(pred[12]{0:T(512)(128)(4,1)} %copy-done.25) | copy-start | bytes 40
  (39 other events, 895.6 us)
Sparse Core Ops, SparseCore 0:
  19.3 74.3 all-reduce.9
  97.6 58.1 all-gather.4
  311.7 72.1 all-reduce.11
  387.2 58.1 all-gather.6
  827.7 73.2 all-reduce.13
  904.8 58.1 all-gather.8
  1475.1 73.0 all-reduce.15
  1554.1 125.3 all-reduce.17
  1683.4 60.0 all-gather.10
where the time goes:
time: 1990 us; the launch traced here: 1960 us
  local copies, waits for them, and re-layouts  973 us (49%)
  waiting for transfers between devices  499 us (25%)
  other arithmetic  236 us (12%)
  matrix products  179 us (9%)
  blocking collectives  39.3 us (2%)
  starting transfers between devices  21.1 us (1%)
    psum x4, waiting for transfers between devices, place_lines(): own_lines = lax.psum(placed.astype(jnp.bfloat16), 'tile')  248 us
    conv_general_dilated x16, local copies, waits for them, and re-layouts, convolve(): lax.conv_general_dilated(padded, weight, (1, 1), 'VALID', dimension_numbe...  238 us
    all_gather x4, waiting for transfers between devices, partner_pieces(): gathered = lax.all_gather(front, ('face', 'tile'), axis=3, tiled=True)  172 us
    scatter-add x2, local copies, waits for them, and re-layouts, unfold_strip(): interior.at[:, :, -1, :]  147 us
    unnamed x128, local copies, waits for them, and re-layouts  125 us
    conv_general_dilated x4, matrix products, convolve(): lax.conv_general_dilated(padded, weight, (1, 1), 'VALID', dimension_numbe...  89.7 us
    conv_general_dilated x2, matrix products, weight_grad(): lax.conv_general_dilated(padded, cotangent, (1, 1), 'VALID', dimension_nu...  89.7 us
    scatter-add x2, local copies, waits for them, and re-layouts, unfold_strip(): interior.at[:, :, 0, :]  87.2 us
  transfers between devices with their start and end apart: 17, of which 11 were waited for; matrix products, arithmetic and copies ran while one was open for 13% of the time, Pallas kernels for 0%

commit v1 on v0

v1 whole, which is shorter than its diff:
```python
import functools

import jax
import jax.numpy as jnp
from jax import lax
from jax.experimental import pallas as pl
from jax.experimental.pallas import tpu as pltpu
from jax.sharding import PartitionSpec as P

INV_ROOT_TWO = 0.7071067811865476
INV_ROOT_TWO_PI = 0.3989422804014327
F32 = jnp.float32
BF16 = jnp.bfloat16
LANES = 128
MESH_ID = pl.DeviceIdType.MESH


def gelu_pair(values):
    normal_cdf = 0.5 * (1.0 + lax.erf(values * INV_ROOT_TWO))
    normal_pdf = jnp.exp(-0.5 * values * values) * INV_ROOT_TWO_PI
    return (values * normal_cdf, normal_cdf + values * normal_pdf)


def lane_index(channels):
    return lax.broadcasted_iota(jnp.int32, (channels, LANES), 1)


def build_patches(x_ref, halo_ref, ghost_ref, patch_ref):
    rows, channels, width = x_ref.shape
    lane = lane_index(channels)

    def put(p, row):
        wide = row.astype(F32)
        left = pltpu.roll(wide, 1, 1)
        right = pltpu.roll(wide, width - 1, 1)
        if ghost_ref is None:
            west = east = jnp.zeros((channels, LANES), F32)
        else:
            west = pltpu.roll(ghost_ref[0], lax.rem(LANES - p, LANES), 1)
            east = pltpu.roll(ghost_ref[1], LANES - 1 - p, 1)
        left = jnp.concatenate([jnp.where(lane == 0, west, left[:, :LANES]), left[:, LANES:]], axis=1)
        right = jnp.concatenate(
            [right[:, :-LANES], jnp.where(lane == LANES - 1, east, right[:, -LANES:])], axis=1
        )
        patch_ref[p, 0:channels] = left.astype(BF16)
        patch_ref[p, channels : 2 * channels] = row
        patch_ref[p, 2 * channels : 3 * channels] = right.astype(BF16)

    put(jnp.int32(0), halo_ref[0])
    put(jnp.int32(rows + 1), halo_ref[1])

    def step(r, carry):
        for i in range(2):
            put(2 * r + i + 1, x_ref[2 * r + i])
        return carry

    lax.fori_loop(0, rows // 2, step, 0)


def patch_rows(patch_ref, r):
    _, depth, width = patch_ref.shape
    return patch_ref[pl.ds(r, 3)].reshape(3 * depth, width)


def conv_row(w, patch_ref, r):
    return jnp.dot(w, patch_rows(patch_ref, r), preferred_element_type=F32)


def keep_columns(edge_ref, r, row, lane):
    channels, width = row.shape
    edge_ref[0] = jnp.where(lane == r, pltpu.roll(row[:, :LANES], r, 1), edge_ref[0])
    edge_ref[1] = jnp.where(
        lane == r, pltpu.roll(row[:, -LANES:], lax.rem(r + 1, LANES), 1), edge_ref[1]
    )


def over_rows(rows, body):
    group = 4

    def step(s, carry):
        for i in range(group):
            body(s * group + i)
        return carry

    lax.fori_loop(0, rows // group, step, 0)


def first_kernel(x_ref, halo_ref, ghost_ref, w_ref, b_ref, hidden_ref, slope_ref, edge_ref, patch_ref):
    rows, channels, width = x_ref.shape
    build_patches(x_ref, halo_ref, ghost_ref, patch_ref)
    edge_ref[...] = jnp.zeros_like(edge_ref)
    lane = lane_index(channels)
    w = w_ref[...]

    def body(r):
        pre = conv_row(w, patch_ref, r) + b_ref[...]
        value, slope = gelu_pair(pre)
        slope_ref[r] = slope
        hidden_ref[r] = value.astype(BF16)
        keep_columns(edge_ref, r, value, lane)

    over_rows(rows, body)


def add_products(gw_ref, g_row, patch_ref, r):
    gw_ref[...] += lax.dot_general(
        patch_rows(patch_ref, r), g_row, (((1,), (1,)), ((), ())), preferred_element_type=F32
    )


def second_kernel(
    x_ref, halo_ref, ghost_ref, og_ref, w_ref, b_ref, out_ref, g_ref, edge_ref, gw_ref, gb_ref, patch_ref
):
    rows, channels, width = x_ref.shape
    build_patches(x_ref, halo_ref, ghost_ref, patch_ref)
    edge_ref[...] = jnp.zeros_like(edge_ref)

    @pl.when(pl.program_id(0) == 0)
    def _():
        gw_ref[...] = jnp.zeros_like(gw_ref)
        gb_ref[...] = jnp.zeros_like(gb_ref)

    lane = lane_index(channels)
    w = w_ref[...]

    def body(r):
        pre = conv_row(w, patch_ref, r) + b_ref[...]
        value, slope = gelu_pair(pre)
        out_ref[r] = value.astype(BF16)
        grad = (og_ref[r].astype(F32) * slope).astype(BF16)
        g_ref[r] = grad
        wide = grad.astype(F32)
        gb_ref[...] += wide
        keep_columns(edge_ref, r, wide, lane)
        add_products(gw_ref, grad, patch_ref, r)

    over_rows(rows, body)


def add_edges(total, r, rows, col_ref, row_ref, lane):
    west = pltpu.roll(col_ref[0], lax.rem(LANES - r, LANES), 1)
    east = pltpu.roll(col_ref[1], LANES - 1 - r, 1)
    zero = jnp.zeros_like(west)
    parts = [total[:, i : i + LANES] for i in range(0, total.shape[1], LANES)]
    parts[0] = parts[0] + jnp.where(lane == 0, west, zero)
    parts[-1] = parts[-1] + jnp.where(lane == LANES - 1, east, zero)
    total = jnp.concatenate(parts, axis=1)
    north = jnp.where(r == 0, row_ref[0], jnp.zeros_like(row_ref[0]))
    south = jnp.where(r == rows - 1, row_ref[1], jnp.zeros_like(row_ref[1]))
    return total + north + south


def third_kernel(
    g_ref, halo_ref, col_ref, row_ref, slope_ref, x_ref, xhalo_ref, xghost_ref, w_ref,
    out_ref, edge_ref, gw_ref, gb_ref, patch_ref, xpatch_ref,
):
    rows, channels, width = g_ref.shape
    build_patches(g_ref, halo_ref, None, patch_ref)
    build_patches(x_ref, xhalo_ref, xghost_ref, xpatch_ref)
    edge_ref[...] = jnp.zeros_like(edge_ref)

    @pl.when(pl.program_id(0) == 0)
    def _():
        gw_ref[...] = jnp.zeros_like(gw_ref)
        gb_ref[...] = jnp.zeros_like(gb_ref)

    lane = lane_index(channels)
    w = w_ref[...]

    def body(r):
        total = add_edges(conv_row(w, patch_ref, r), r, rows, col_ref, row_ref, lane)
        grad = (total * slope_ref[r]).astype(BF16)
        out_ref[r] = grad
        wide = grad.astype(F32)
        gb_ref[...] += wide
        keep_columns(edge_ref, r, wide, lane)
        add_products(gw_ref, grad, xpatch_ref, r)

    over_rows(rows, body)


def fourth_kernel(g_ref, halo_ref, col_ref, row_ref, w_ref, out_ref, patch_ref):
    rows, channels, width = g_ref.shape
    build_patches(g_ref, halo_ref, None, patch_ref)
    lane = lane_index(channels)
    w = w_ref[...]

    def body(r):
        total = add_edges(conv_row(w, patch_ref, r), r, rows, col_ref, row_ref, lane)
        out_ref[r] = total.astype(BF16)

    over_rows(rows, body)


def per_face(shape):
    tail = len(shape) - 1
    return pl.BlockSpec((None,) + tuple(shape[1:]), lambda f: (f,) + (0,) * tail)


def whole(shape):
    return pl.BlockSpec(tuple(shape), lambda f: (0,) * len(shape))


def run_faces(kernel, faced, shared, faced_outs, shared_outs, patches, flops):
    faces = faced[0].shape[0]
    rows, channels, width = faced[0].shape[1:]
    outs = [jax.ShapeDtypeStruct(s, d) for s, d in faced_outs + shared_outs]
    return pl.pallas_call(
        kernel,
        grid=(faces,),
        in_specs=[per_face(a.shape) for a in faced] + [whole(a.shape) for a in shared],
        out_specs=[per_face(s) for s, _ in faced_outs] + [whole(s) for s, _ in shared_outs],
        out_shape=outs,
        scratch_shapes=[pltpu.VMEM((rows + 2, 3 * channels, width), BF16)] * patches,
        compiler_params=pltpu.CompilerParams(vmem_limit_bytes=40 << 20),
        cost_estimate=pl.CostEstimate(flops=flops, bytes_accessed=10**7, transcendentals=10**6),
    )(*faced, *shared)


def flipped_bit(i, bit):
    return i + bit - 2 * bit * lax.rem(lax.div(i, bit), 2)


def gather_kernel(faces, tiles, we_ref, ns_ref, we_all, ns_all, tsend, trecv, nsend, nrecv, fsend, frecv, gsend, grecv):
    face = lax.axis_index("face")
    tile = lax.axis_index("tile")
    tile_bits = [1 << b for b in range(tiles.bit_length() - 1)]
    face_bits = [1 << b for b in reversed(range(faces.bit_length() - 1))]
    barrier = pltpu.get_barrier_semaphore()
    for bit in tile_bits:
        pl.semaphore_signal(barrier, inc=1, device_id=(face, flipped_bit(tile, bit)), device_id_type=MESH_ID)
    for bit in face_bits:
        pl.semaphore_signal(barrier, inc=1, device_id=(flipped_bit(face, bit), tile), device_id_type=MESH_ID)
    we_all[face, tile] = we_ref[...]

    @pl.when(tile == 0)
    def _():
        ns_all[face, 0] = ns_ref[0]

    @pl.when(tile == tiles - 1)
    def _():
        ns_all[face, 1] = ns_ref[1]

    pl.semaphore_wait(barrier, len(tile_bits) + len(face_bits))
    for i, bit in enumerate(tile_bits):
        partner = (face, flipped_bit(tile, bit))
        block = we_all.at[face, pl.ds(lax.div(tile, bit) * bit, bit)]
        copy = pltpu.make_async_remote_copy(block, block, tsend.at[i], trecv.at[i], partner, MESH_ID)
        copy.start()
        lines = []
        for side, place in enumerate((tile, tiles - 1 - tile)):
            line = ns_all.at[face, side]
            send = pltpu.make_async_remote_copy(
                line, line, nsend.at[side, i], nrecv.at[side, i], partner, MESH_ID
            )
            lines.append((place, send))

            @pl.when(place < bit)
            def _():
                send.start()

        copy.wait()
        for place, send in lines:

            @pl.when(place < bit)
            def _():
                send.wait_send()

            @pl.when((place >= bit) & (place < 2 * bit))
            def _():
                send.wait_recv()

    held = [face]
    slot = 0
    for bit in face_bits:
        partner = (flipped_bit(face, bit), tile)
        copies = []
        for h in held:
            block = we_all.at[h]
            copies.append(pltpu.make_async_remote_copy(block, block, fsend.at[slot], frecv.at[slot], partner, MESH_ID))
            lines = ns_all.at[h]
            copies.append(pltpu.make_async_remote_copy(lines, lines, gsend.at[slot], grecv.at[slot], partner, MESH_ID))
            slot += 1
        for copy in copies:
            copy.start()
        for copy in copies:
            copy.wait()
        held = held + [flipped_bit(h, bit) for h in held]


def gather_lines(we, ns):
    faces, tiles = lax.axis_size("face"), lax.axis_size("tile")
    steps = tiles.bit_length() - 1
    dma = pltpu.SemaphoreType.DMA
    return pl.pallas_call(
        functools.partial(gather_kernel, faces, tiles),
        in_specs=[pl.BlockSpec(memory_space=pltpu.VMEM)] * 2,
        out_specs=[pl.BlockSpec(memory_space=pltpu.VMEM)] * 2,
        out_shape=[
            jax.ShapeDtypeStruct((faces, tiles) + we.shape, BF16),
            jax.ShapeDtypeStruct((faces,) + ns.shape, BF16),
        ],
        scratch_shapes=[
            dma((steps,)), dma((steps,)), dma((2, steps)), dma((2, steps)),
            dma((faces,)), dma((faces,)), dma((faces,)), dma((faces,)),
        ],
        compiler_params=pltpu.CompilerParams(collective_id=0, has_side_effects=True),
    )(we, ns)


def exchange(north, south, west, east, links):
    faces_dev, channels, side = north.shape
    seg = west.shape[2]
    we = jnp.stack([west, east], axis=1)
    we = jnp.transpose(we, (2, 0, 1, 3)).reshape(channels, faces_dev * 2 * seg)
    we_all, ns_all = gather_lines(we, jnp.stack([north, south]))
    groups, tiles = we_all.shape[:2]
    we_all = we_all.reshape(groups, tiles, channels, faces_dev, 2, seg)
    we_all = jnp.transpose(we_all, (0, 3, 4, 2, 1, 5)).reshape(groups, faces_dev, 2, channels, side)
    ns_all = jnp.transpose(ns_all, (0, 2, 1, 3, 4))
    lines = jnp.concatenate([ns_all, we_all], axis=2).reshape(groups * faces_dev * 4, channels, side)
    index = (links[:, :, 0] * 4 + links[:, :, 1]).reshape(-1)
    picked = jnp.take(lines, index, axis=0, mode="clip").reshape(faces_dev, 4, channels, side)
    return jnp.where((links[:, :, 2] == 1)[:, :, None, None], picked[..., ::-1], picked)


def halo(first, last):
    count = lax.axis_size("tile")
    down = [(i, i + 1) for i in range(count - 1)]
    up = [(i + 1, i) for i in range(count - 1)]
    return lax.ppermute(last, "tile", down), lax.ppermute(first, "tile", up)


def fill(north, south, west, east, links, corners, pos, count):
    seg = west.shape[2]
    above, below = halo(north, south)
    ghosts = exchange(north, south, west, east, links)
    code = (corners == 0)[:, :, None]
    gn, gs, gw, ge = (ghosts[:, i] for i in range(4))
    nw = jnp.where(code[:, 0], gn[:, :, 0], gw[:, :, 0])
    ne = jnp.where(code[:, 1], gn[:, :, -1], ge[:, :, 0])
    sw = jnp.where(code[:, 2], gs[:, :, 0], gw[:, :, -1])
    se = jnp.where(code[:, 3], gs[:, :, -1], ge[:, :, -1])
    west_all = jnp.concatenate([nw[:, :, None], gw, sw[:, :, None]], axis=2)
    east_all = jnp.concatenate([ne[:, :, None], ge, se[:, :, None]], axis=2)
    columns = jnp.stack([west_all, east_all], axis=1)
    columns = lax.dynamic_slice_in_dim(columns, pos * seg, seg + 2, 3).astype(F32)
    columns = jnp.pad(columns, ((0, 0), (0, 0), (0, 0), (0, LANES - seg - 2)))
    top = jnp.where(pos == 0, gn, above)
    bottom = jnp.where(pos == count - 1, gs, below)
    return jnp.stack([top, bottom], axis=1), columns


def line_product(weights, line):
    size = line.shape[2]
    padded = jnp.pad(line, ((0, 0), (0, 0), (2, 2)))
    stacked = jnp.concatenate([padded[:, :, 2 - t : 2 - t + size + 2] for t in range(3)], axis=1)
    flat = jnp.transpose(weights, (2, 0, 1)).reshape(-1, weights.shape[1])
    return jnp.einsum("kc,fkq->fcq", flat, stacked, preferred_element_type=F32)


def unfold_edges(north, south, west, east, weight, links, corners, pos, count):
    seg = west.shape[2]
    above, below = halo(north, south)
    rows = jnp.stack([above, below], axis=1)
    west = jnp.concatenate([above[:, :, :1], west, below[:, :, :1]], axis=2)
    east = jnp.concatenate([above[:, :, -1:], east, below[:, :, -1:]], axis=2)
    gn = line_product(weight[:, :, 0, :], north)
    gs = line_product(weight[:, :, 2, :], south)
    gw = line_product(weight[:, :, :, 0], west)[:, :, 2:-2]
    ge = line_product(weight[:, :, :, 2], east)[:, :, 2:-2]
    code = corners[:, :, None]
    zero = jnp.zeros((), F32)
    at_top, at_bottom = pos == 0, pos == count - 1
    nw, ne, sw, se = gn[:, :, :1], gn[:, :, -1:], gs[:, :, :1], gs[:, :, -1:]
    keep = lambda i, corner: jnp.where(code[:, i, :, None] == 0, corner, zero)
    give = lambda i, corner, here: jnp.where((code[:, i, :, None] == 1) & here, corner, zero)
    ends = lambda lo, hi, n: jnp.pad(lo, ((0, 0), (0, 0), (0, n - 1))) + jnp.pad(hi, ((0, 0), (0, 0), (n - 1, 0)))
    side = north.shape[2]
    gn_line = gn[:, :, 1:-1] + ends(keep(0, nw), keep(1, ne), side)
    gs_line = gs[:, :, 1:-1] + ends(keep(2, sw), keep(3, se), side)
    gw_line = gw + ends(give(0, nw, at_top), give(2, sw, at_bottom), seg)
    ge_line = ge + ends(give(1, ne, at_top), give(3, se, at_bottom), seg)
    ghosts = exchange(
        gn_line.astype(BF16), gs_line.astype(BF16), gw_line.astype(BF16), ge_line.astype(BF16), links
    ).astype(F32)
    columns = lax.dynamic_slice_in_dim(ghosts[:, 2:], pos * seg, seg, 3)
    columns = jnp.pad(columns, ((0, 0), (0, 0), (0, 0), (0, LANES - seg)))
    edges = jnp.stack(
        [jnp.where(at_top, ghosts[:, 0], zero), jnp.where(at_bottom, ghosts[:, 1], zero)], axis=1
    )
    return rows, columns, edges


def body(field_in, out_grad, weight_first, bias_first, weight_second, bias_second, face_links, corner_rules):
    count = lax.axis_size("tile")
    pos = lax.axis_index("tile")
    face_pos = lax.axis_index("face")
    faces, channels, rows, side = field_in.shape
    links = lax.dynamic_slice_in_dim(face_links, face_pos * faces, faces, 0)
    corners = lax.dynamic_slice_in_dim(corner_rules, face_pos * faces, faces, 0)
    swap = lambda a: jnp.transpose(a, (0, 2, 1, 3))
    ahead = lambda w: jnp.transpose(w, (0, 2, 3, 1)).reshape(channels, 9 * channels)
    behind = lambda w: jnp.transpose(w[:, :, ::-1, ::-1], (1, 2, 3, 0)).reshape(channels, 9 * channels)
    flops = 2 * 9 * channels * channels * faces * rows * side
    full = (faces, rows, channels, side)
    edge_out = ((faces, 2, channels, LANES), F32)
    sums = [((9 * channels, channels), F32), ((channels, side), F32)]

    x = swap(field_in)
    og = swap(out_grad)
    xhalo, xghost = fill(
        field_in[:, :, 0], field_in[:, :, -1], field_in[:, :, :, 0], field_in[:, :, :, -1],
        links, corners, pos, count,
    )
    hidden, slope, hedge = run_faces(
        first_kernel, [x, xhalo, xghost], [ahead(weight_first), bias_first[:, None]],
        [(full, BF16), (full, F32), edge_out], [], 1, flops,
    )

    def sides(edge):
        return edge[:, 0, :, :rows].astype(BF16), edge[:, 1, :, :rows].astype(BF16)

    hhalo, hghost = fill(hidden[:, 0], hidden[:, -1], *sides(hedge), links, corners, pos, count)
    output, g2, gedge, gw2, gb2 = run_faces(
        second_kernel, [hidden, hhalo, hghost, og], [ahead(weight_second), bias_second[:, None]],
        [(full, BF16), (full, BF16), edge_out], sums, 1, 2 * flops,
    )
    ghalo, gcol, grow = unfold_edges(
        g2[:, 0], g2[:, -1], *sides(gedge), weight_second, links, corners, pos, count
    )
    g1, fedge, gw1, gb1 = run_faces(
        third_kernel, [g2, ghalo, gcol, grow, slope, x, xhalo, xghost], [behind(weight_second)],
        [(full, BF16), edge_out], sums, 2, 2 * flops,
    )
    fhalo, fcol, frow = unfold_edges(
        g1[:, 0], g1[:, -1], *sides(fedge), weight_first, links, corners, pos, count
    )
    (grad_field,) = run_faces(
        fourth_kernel, [g1, fhalo, fcol, frow], [behind(weight_first)], [(full, BF16)], [], 1, flops
    )
    packed = jnp.concatenate(
        [gw1, gw2, jnp.sum(gb1, axis=1)[None], jnp.sum(gb2, axis=1)[None]], axis=0
    )
    packed = lax.psum(packed, ("face", "tile")) / side
    depth = 9 * channels
    shaped = lambda g: jnp.transpose(g.reshape(3, 3, channels, channels), (3, 2, 0, 1))
    return (
        swap(output),
        swap(grad_field),
        shaped(packed[:depth]),
        packed[2 * depth],
        shaped(packed[depth : 2 * depth]),
        packed[2 * depth + 1],
    )


def solution(mesh):
    cells = P("face", None, "tile", None)
    return jax.shard_map(
        body,
        mesh=mesh,
        in_specs=(cells, cells, P(), P(), P(), P(), P(), P()),
        out_specs=(cells, cells, P(), P(), P(), P()),
        check_vma=False,
    )
```

time: 1990 us -> 433 us (0.22); the launches traced: 1960 us -> 430 us
  local copies, waits for them, and re-layouts: 973 us -> 103 us
  waiting for transfers between devices: 499 us -> 72.6 us
  other arithmetic: 236 us -> 17.6 us
  Pallas kernels: 0 us -> 200 us
  matrix products: 179 us -> 1.68 us
  blocking collectives: 39.3 us -> 0 us
    scatter-add x20 -> x0, local copies, waits for them, and re-layouts: 239 us -> none  [the longest x2 147 us: unfold_strip(): interior.at[:, :, -1, :]]
    conv_general_dilated x16 -> x0, local copies, waits for them, and re-layouts: 238 us -> none  [convolve(): lax.conv_general_dilated(padded, weight, (1, 1), 'VALID', dimension_numbe...]
    psum x5 -> x1, waiting for transfers between devices: 303 us -> 65.3 us  [body(): packed = lax.psum(packed, ('face', 'tile')) / side]
    pallas_call x0 -> x8, Pallas kernels: none -> 200 us  [the longest x4 117 us: gather_lines(): pl.pallas_call(functools.partial(gather_kernel, faces, tiles), in_specs=[...]
    conv_general_dilated x6 -> x0, matrix products: 179 us -> none  [the longest x4 89.7 us: convolve(): lax.conv_general_dilated(padded, weight, (1, 1), 'VALID', dimension_numbe...]
    slice x20 -> x23, local copies, waits for them, and re-layouts: 184 us -> 12.1 us  [the longest x1 3.75 us: body(): field_in[:, :, :, 0]]
    all_gather x4 -> x0, waiting for transfers between devices: 172 us -> none  [partner_pieces(): gathered = lax.all_gather(front, ('face', 'tile'), axis=3, tiled=True)]
    unnamed x128 -> x118, local copies, waits for them, and re-layouts: 125 us -> 33.9 us
  transfers between devices with their start and end apart: 17 -> 9, of which waited for: 11 -> 4; matrix products, arithmetic and copies ran while one was open for 13% -> 15% of each run, Pallas kernels for 0% -> 17%
where the time goes in v1:
time: 433 us; the launch traced here: 430 us
  Pallas kernels  200 us (46%)
  local copies, waits for them, and re-layouts  103 us (24%)
  waiting for transfers between devices  72.6 us (17%)
  starting transfers between devices  19.9 us (5%)
  other arithmetic  17.6 us (4%)
  between operations  15.5 us (4%)
    pallas_call x4, Pallas kernels, gather_lines(): pl.pallas_call(functools.partial(gather_kernel, faces, tiles), in_specs=[...  117 us
    pallas_call x4, Pallas kernels, run_faces(): pl.pallas_call(kernel, grid=(faces,), in_specs=[per_face(a.shape) for a i...  82.7 us
    psum x1, waiting for transfers between devices, body(): packed = lax.psum(packed, ('face', 'tile')) / side  65.3 us
    unnamed x118, local copies, waits for them, and re-layouts  33.9 us
    reshape x8, local copies, waits for them, and re-layouts, exchange(): jnp.transpose(we_all, (0, 3, 4, 2, 1, 5))  27.2 us
    ppermute x8, starting transfers between devices, halo(): return (lax.ppermute(last, 'tile', down), lax.ppermute(first, 'tile', up))  19.8 us
    pallas_call x4, local copies, waits for them, and re-layouts, gather_lines(): pl.pallas_call(functools.partial(gather_kernel, faces, tiles), in_specs=[...  10.2 us
  transfers between devices with their start and end apart: 9, of which 4 were waited for; matrix products, arithmetic and copies ran while one was open for 15% of the time, Pallas kernels for 17%

profile of v1, /device:TPU:0, one launch (start us, length us, event | category | flops | bytes accessed | tf_op | source)
XLA Modules:
  0.0 430.0 jit_solution(2474072636087159879)
XLA Ops:
  9.3 5.5 %collective-permute-start = (bf16[3,48,256]{2,1,0:T(8,128)(2,1)}, bf16[3,48,256]{2,1,0:T(8,128)(2,1)}, u32[]{:S(2)}, u32[]{:S(2)}) collective-permute-start(bf16[3,48,256]{2,1,0:T(8,128)(2,1)} %bitcast.265), channel_id=1, source_target_pairs={{0,1},{1,2},{2,3},{3,4},{4,5},{5,6},{6,7},{8,9},{9,10},{10,11},{11... | collective-permute-start | bytes 221192 | tf_op jit(solution)/shard_map/ppermute | solution.py:331
  16.8 3.8 fusion.72
  25.5 2.5 copy.344
  28.0 2.5 copy.345
  32.9 32.3 %shard_map.127 = (bf16[4,8,48,192]{3,2,1,0:T(8,128)(2,1)}, bf16[4,2,3,48,256]{4,3,2,1,0:T(8,128)(2,1)}) custom-call(bf16[48,192]{1,0:T(8,128)(2,1)} %copy.235.we_ref, bf16[2,3,48,256]{3,2,1,0:T(8,128)(2,1)} %pad_maximum_fusion.7.ns_ref), custom_call_target="tpu_custom_call" | custom-call | tf_op jit(solution)/shard_map/pallas_call | solution.py:295
  65.1 2.5 copy.236
  67.6 4.1 copy.326
  71.7 3.4 reshape.299
  82.7 4.4 %copy.366 = bf16[3,48,32,256]{3,1,2,0:T(8,128)(2,1)} copy(bf16[3,48,32,256]{3,2,1,0:T(8,128)(2,1)} %param.9) | data formatting | bytes 4718592 | tf_op args[1]
  89.5 14.8 %shard_map.128 = (bf16[3,32,48,256]{3,2,1,0:T(8,128)(2,1)S(1)}, f32[3,32,48,256]{3,2,1,0:T(8,128)S(1)}, f32[3,2,48,128]{3,2,1,0:T(8,128)S(1)}) custom-call(bf16[3,32,48,256]{3,2,1,0:T(8,128)(2,1)S(1)} %bitcast.267, bf16[3,2,48,256]{3,2,1,0:T(8,128)(2,1)S(1)} %copy.246.halo_ref.xhalo_ref, f32[3,2,48,128]{3,2,1,0:T(8,128)S(1)} %copy.247.ghost_ref.xghost_ref, ...), custom_call_target="tpu_custom_call" | custom-call | flops 1019215872 | bytes 10000000 | tf_op jit(solution)/shard_map/pallas_call | solution.py:208
  104.3 2.2 copy-done
  110.0 27.3 %shard_map.129 = (bf16[4,8,48,192]{3,2,1,0:T(8,128)(2,1)}, bf16[4,2,3,48,256]{4,3,2,1,0:T(8,128)(2,1)}) custom-call(bf16[48,192]{1,0:T(8,128)(2,1)} %copy.252.we_ref, bf16[2,3,48,256]{3,2,1,0:T(8,128)(2,1)} %pad_maximum_fusion.9.ns_ref), custom_call_target="tpu_custom_call" | custom-call | tf_op jit(solution)/shard_map/pallas_call | solution.py:295
  137.3 2.6 copy.253
  139.9 4.1 copy.327
  144.0 3.4 reshape.300
  156.1 4.5 %collective-permute-done.3 = bf16[3,48,256]{2,1,0:T(8,128)(2,1)S(1)} collective-permute-done((bf16[3,48,256]{2,1,0:T(8,128)(2,1)S(1)}, bf16[3,48,256]{2,1,0:T(8,128)(2,1)S(1)}, u32[]{:S(2)}, u32[]{:S(2)}) %collective-permute-start.3) | collective-permute-done | bytes 73760 | tf_op jit(solution)/shard_map/ppermute | solution.py:331
  162.4 26.2 %shard_map.130 = (bf16[3,32,48,256]{3,2,1,0:T(8,128)(2,1)S(1)}, bf16[3,32,48,256]{3,2,1,0:T(8,128)(2,1)S(1)}, f32[3,2,48,128]{3,2,1,0:T(8,128)S(1)}, f32[432,48]{1,0:T(8,128)S(1)}, f32[48,256]{1,0:T(8,128)S(1)}) custom-call(bf16[3,32,48,256]{3,2,1,0:T(8,128)(2,1)S(1)} %copy-done.9, bf16[3,2,48,256]{3,2,1,0:T(8,128)(2,1)S(1)} %copy.262.halo_ref, ...), custom_call_target="tpu_custom_call" | custom-call | flops 2038431744 | bytes 10000000 | tf_op jit(solution)/shard_map/pallas_call | solution.py:208
  192.2 4.6 %collective-permute-start.4 = (bf16[3,48,256]{2,1,0:T(8,128)(2,1)S(1)}, bf16[3,48,256]{2,1,0:T(8,128)(2,1)S(1)}, u32[]{:S(2)}, u32[]{:S(2)}) collective-permute-start(bf16[3,48,256]{2,1,0:T(8,128)(2,1)S(1)} %get-tuple-element.88), channel_id=1, source_target_pairs={{0,1},{1,2},{2,3},{3,4},{4,5},{5,6},{6,7},{8,9},{9,10},{10,11},{11... | collective-permute-start | bytes 221192 | tf_op jit(solution)/shard_map/ppermute | solution.py:331
  200.6 4.0 copy.306
  209.6 29.5 %shard_map.131 = (bf16[4,8,48,192]{3,2,1,0:T(8,128)(2,1)}, bf16[4,2,3,48,256]{4,3,2,1,0:T(8,128)(2,1)}) custom-call(bf16[48,192]{1,0:T(8,128)(2,1)} %copy.277.we_ref, bf16[2,3,48,256]{3,2,1,0:T(8,128)(2,1)} %pad_maximum_fusion.12.ns_ref), custom_call_target="tpu_custom_call" | custom-call | tf_op jit(solution)/shard_map/pallas_call | solution.py:295
  239.1 2.6 copy.278
  241.7 4.1 copy.332
  245.8 3.4 reshape.301
  255.6 2.3 copy-done.1
  257.9 30.0 %shard_map.132 = (bf16[3,32,48,256]{3,2,1,0:T(8,128)(2,1)S(1)}, f32[3,2,48,128]{3,2,1,0:T(8,128)S(1)}, f32[432,48]{1,0:T(8,128)S(1)}, f32[48,256]{1,0:T(8,128)S(1)}) custom-call(bf16[3,32,48,256]{3,2,1,0:T(8,128)(2,1)S(1)} %copy-done.3, bf16[3,2,48,256]{3,2,1,0:T(8,128)(2,1)S(1)} %pad_maximum_fusion.11.halo_ref, f32[3,2,48,128]{3,2,1,0:T(8,128)S(1)} %pad.112.col_ref, ...), custom_call_target="tpu_custom_call" | custom-call | flops 2038431744 | bytes 10000000 | tf_op jit(solution)/shard_map/pallas_call | solution.py:208
  289.6 3.1 collective-permute-start.6
  301.1 28.0 %shard_map.133 = (bf16[4,8,48,192]{3,2,1,0:T(8,128)(2,1)}, bf16[4,2,3,48,256]{4,3,2,1,0:T(8,128)(2,1)}) custom-call(bf16[48,192]{1,0:T(8,128)(2,1)} %copy.296.we_ref, bf16[2,3,48,256]{3,2,1,0:T(8,128)(2,1)} %pad_maximum_fusion.14.ns_ref), custom_call_target="tpu_custom_call" | custom-call | tf_op jit(solution)/shard_map/pallas_call | solution.py:295
  329.1 2.5 copy.297
  331.6 3.0 copy.338
  340.3 11.7 %shard_map.134 = bf16[3,32,48,256]{3,2,1,0:T(8,128)(2,1)S(1)} custom-call(bf16[3,32,48,256]{3,2,1,0:T(8,128)(2,1)S(1)} %copy-done.5, bf16[3,2,48,256]{3,2,1,0:T(8,128)(2,1)S(1)} %pad_maximum_fusion.13.halo_ref, f32[3,2,48,128]{3,2,1,0:T(8,128)S(1)} %pad.125.col_ref, f32[3,2,48,256]{3,2,1,0:T(8,128)S(1)} %pad_maximum_fusion.5.row_ref, ...), custom_call_target="tpu_custom_call" | custom-call | flops 1019215872 | bytes 10000000 | tf_op jit(solution)/shard_map/pallas_call | solution.py:208
  352.0 2.2 copy.307
  354.3 65.3 %all-reduce.30.cloned.1.call-done = f32[866,48]{0,1:T(8,128)} async-done(((f32[866,48]{0,1:T(8,128)}), f32[866,48]{0,1:T(8,128)}) %all-reduce.30.cloned.1.call-update) | async-done | bytes 166288 | tf_op jit(solution)/shard_map/psum | solution.py:445
  (275 shorter events, 72.0 us)
Async XLA Ops:
  7.2 412.5 %all-reduce.30.cloned.1.call-start = ((), (), s32[]{:S(2)}) async-start(), calls=%async_computation | async-start | bytes 344064 | tf_op jit(solution)/shard_map/psum | solution.py:445
  9.3 79.2 %collective-permute-start = (bf16[3,48,256]{2,1,0:T(8,128)(2,1)}, bf16[3,48,256]{2,1,0:T(8,128)(2,1)}, u32[]{:S(2)}, u32[]{:S(2)}) collective-permute-start(bf16[3,48,256]{2,1,0:T(8,128)(2,1)} %bitcast.265), channel_id=1, source_target_pairs={{0,1},{1,2},{2,3},{3,4},{4,5},{5,6},{6,7},{8,9},{9,10},{10,11},{11... | collective-permute-start | bytes 221192 | tf_op jit(solution)/shard_map/ppermute | solution.py:331
  15.5 73.1 %collective-permute-start.1 = (bf16[3,48,256]{2,1,0:T(8,128)(2,1)}, bf16[3,48,256]{2,1,0:T(8,128)(2,1)}, u32[]{:S(2)}, u32[]{:S(2)}) collective-permute-start(bf16[3,48,256]{2,1,0:T(8,128)(2,1)} %bitcast.233.clone.2), channel_id=1, source_target_pairs={{1,0},{2,1},{3,2},{4,3},{5,4},{6,5},{7,6},{9,8},{10,9},{11,10},{12... | collective-permute-start | bytes 221192 | tf_op jit(solution)/shard_map/ppermute | solution.py:331
  16.8 3.8 copy-start.10
  77.4 4.0 copy-start.51
  82.7 69.3 %copy-start.33 = (pred[3,4,1]{1,0,2:T(4,128)(4,1)}, pred[3,4,1]{1,0,2:T(4,128)(4,1)S(1)}, u32[]{:S(2)}) copy-start(pred[3,4,1]{1,0,2:T(4,128)(4,1)S(1)} %copy.230) | copy-start | bytes 40
  82.7 4.6 %copy-start.53 = (f32[48]{0:T(128)S(1)}, f32[48]{0:T(128)}, u32[]{:S(2)}) copy-start(f32[48]{0:T(128)} %param.13) | copy-start | bytes 580
  82.7 4.9 %copy-start.13 = (bf16[48,48,3,3]{1,0,3,2:T(8,128)(2,1)S(1)}, bf16[48,48,3,3]{1,0,3,2:T(8,128)(2,1)}, u32[]{:S(2)}) copy-start(bf16[48,48,3,3]{1,0,3,2:T(8,128)(2,1)} %rev.23) | copy-start | bytes 124420
  152.0 8.7 %copy-start.6 = (bf16[3,48,32,256]{3,1,2,0:T(8,128)(2,1)S(1)}, bf16[3,48,32,256]{3,1,2,0:T(8,128)(2,1)}, u32[]{:S(2)}) copy-start(bf16[3,48,32,256]{3,1,2,0:T(8,128)(2,1)} %copy.366) | copy-start | bytes 7077892
  152.1 4.1 collective-permute-start.2
  153.5 7.2 %collective-permute-start.3 = (bf16[3,48,256]{2,1,0:T(8,128)(2,1)S(1)}, bf16[3,48,256]{2,1,0:T(8,128)(2,1)S(1)}, u32[]{:S(2)}, u32[]{:S(2)}) collective-permute-start(bf16[3,48,256]{2,1,0:T(8,128)(2,1)S(1)} %get-tuple-element.91), channel_id=1, source_target_pairs={{1,0},{2,1},{3,2},{4,3},{5,4},{6,5},{7,6},{9,8},{10,9},{11,10},{12... | collective-permute-start | bytes 221192 | tf_op jit(solution)/shard_map/ppermute | solution.py:331
  192.2 14.6 %collective-permute-start.4 = (bf16[3,48,256]{2,1,0:T(8,128)(2,1)S(1)}, bf16[3,48,256]{2,1,0:T(8,128)(2,1)S(1)}, u32[]{:S(2)}, u32[]{:S(2)}) collective-permute-start(bf16[3,48,256]{2,1,0:T(8,128)(2,1)S(1)} %get-tuple-element.88), channel_id=1, source_target_pairs={{0,1},{1,2},{2,3},{3,4},{4,5},{5,6},{6,7},{8,9},{9,10},{10,11},{11... | collective-permute-start | bytes 221192 | tf_op jit(solution)/shard_map/ppermute | solution.py:331
  197.7 9.2 %collective-permute-start.5 = (bf16[3,48,256]{2,1,0:T(8,128)(2,1)S(1)}, bf16[3,48,256]{2,1,0:T(8,128)(2,1)}, u32[]{:S(2)}, u32[]{:S(2)}) collective-permute-start(bf16[3,48,256]{2,1,0:T(8,128)(2,1)S(1)} %get-tuple-element.89), channel_id=1, source_target_pairs={{1,0},{2,1},{3,2},{4,3},{5,4},{6,5},{7,6},{9,8},{10,9},{11,10},{12... | collective-permute-start | bytes 221192 | tf_op jit(solution)/shard_map/ppermute | solution.py:331
  200.5 4.1 copy-start.20
  200.5 4.1 copy-start.21
  200.5 4.1 copy-start.22
  200.5 4.1 copy-start.31
  200.5 4.4 %copy-start.43 = (pred[3]{0:T(512)(128)(4,1)S(1)}, pred[3]{0:T(512)(128)(4,1)}, u32[]{:S(2)}) copy-start(pred[3]{0:T(512)(128)(4,1)} %get-tuple-element.72) | copy-start | bytes 13
  200.5 4.4 %copy-start.45 = (pred[3]{0:T(512)(128)(4,1)S(1)}, pred[3]{0:T(512)(128)(4,1)}, u32[]{:S(2)}) copy-start(pred[3]{0:T(512)(128)(4,1)} %get-tuple-element.74) | copy-start | bytes 13
  200.5 4.4 %copy-start.47 = (pred[3]{0:T(512)(128)(4,1)S(1)}, pred[3]{0:T(512)(128)(4,1)}, u32[]{:S(2)}) copy-start(pred[3]{0:T(512)(128)(4,1)} %get-tuple-element.77) | copy-start | bytes 13
  200.6 4.4 %copy-start.49 = (pred[3]{0:T(512)(128)(4,1)S(1)}, pred[3]{0:T(512)(128)(4,1)}, u32[]{:S(2)}) copy-start(pred[3]{0:T(512)(128)(4,1)} %get-tuple-element.79) | copy-start | bytes 13
  257.9 36.6 %copy-start.23 = (f32[1,48]{0,1:T(8,128)S(1)}, f32[1,48]{0,1:T(8,128)}, u32[]{:S(2)}) copy-start(f32[1,48]{0,1:T(8,128)} %copy.305) | copy-start | bytes 580
  288.0 7.4 %copy-start.27 = (bf16[48,48,1,3]{1,0,3,2:T(8,128)(2,1)S(1)}, bf16[48,48,1,3]{1,0,3,2:T(8,128)(2,1)}, u32[]{:S(2)}) copy-start(bf16[48,48,1,3]{1,0,3,2:T(8,128)(2,1)} %get-tuple-element.138) | copy-start | bytes 41476
  288.0 7.6 %copy-start.44 = (pred[3]{0:T(512)(128)(4,1)S(1)}, pred[3]{0:T(512)(128)(4,1)}, u32[]{:S(2)}) copy-start(pred[3]{0:T(512)(128)(4,1)} %get-tuple-element.72) | copy-start | bytes 13
  288.0 7.6 %copy-start.46 = (pred[3]{0:T(512)(128)(4,1)S(1)}, pred[3]{0:T(512)(128)(4,1)}, u32[]{:S(2)}) copy-start(pred[3]{0:T(512)(128)(4,1)} %get-tuple-element.74) | copy-start | bytes 13
  288.0 7.6 %copy-start.48 = (pred[3]{0:T(512)(128)(4,1)S(1)}, pred[3]{0:T(512)(128)(4,1)}, u32[]{:S(2)}) copy-start(pred[3]{0:T(512)(128)(4,1)} %get-tuple-element.77) | copy-start | bytes 13
  288.0 7.6 %copy-start.50 = (pred[3]{0:T(512)(128)(4,1)S(1)}, pred[3]{0:T(512)(128)(4,1)}, u32[]{:S(2)}) copy-start(pred[3]{0:T(512)(128)(4,1)} %get-tuple-element.79) | copy-start | bytes 13
  289.4 6.3 %copy-start.26 = (bf16[48,48,1,3]{1,0,3,2:T(8,128)(2,1)S(1)}, bf16[48,48,1,3]{1,0,3,2:T(8,128)(2,1)}, u32[]{:S(2)}) copy-start(bf16[48,48,1,3]{1,0,3,2:T(8,128)(2,1)} %get-tuple-element.139) | copy-start | bytes 41476
  289.6 7.5 %collective-permute-start.6 = (bf16[3,48,256]{2,1,0:T(8,128)(2,1)S(1)}, bf16[3,48,256]{2,1,0:T(8,128)(2,1)S(1)}, u32[]{:S(2)}, u32[]{:S(2)}) collective-permute-start(bf16[3,48,256]{2,1,0:T(8,128)(2,1)S(1)} %get-tuple-element.86), channel_id=1, source_target_pairs={{0,1},{1,2},{2,3},{3,4},{4,5},{5,6},{6,7},{8,9},{9,10},{10,11},{11... | collective-permute-start | bytes 221192 | tf_op jit(solution)/shard_map/ppermute | solution.py:331
  292.9 6.2 %collective-permute-start.7 = (bf16[3,48,256]{2,1,0:T(8,128)(2,1)S(1)}, bf16[3,48,256]{2,1,0:T(8,128)(2,1)S(1)}, u32[]{:S(2)}, u32[]{:S(2)}) collective-permute-start(bf16[3,48,256]{2,1,0:T(8,128)(2,1)S(1)} %get-tuple-element.87), channel_id=1, source_target_pairs={{1,0},{2,1},{3,2},{4,3},{5,4},{6,5},{7,6},{9,8},{10,9},{11,10},{12... | collective-permute-start | bytes 221192 | tf_op jit(solution)/shard_map/ppermute | solution.py:331
  296.1 3.8 copy-start.24
  299.1 32.5 %copy-start.14 = (bf16[3,48,256]{2,1,0:T(8,128)(2,1)}, bf16[3,48,256]{2,1,0:T(8,128)(2,1)S(1)}, u32[]{:S(2)}) copy-start(bf16[3,48,256]{2,1,0:T(8,128)(2,1)S(1)} %collective-permute-done.7) | copy-start | bytes 221188
  (31 other events, 53.9 us)
Sparse Core Ops, SparseCore 0:
  295.4 124.1 all-reduce.29

commit v2 on v1

--- a/solution.py
+++ b/solution.py
@@ -221,10 +221,19 @@
     return i + bit - 2 * bit * lax.rem(lax.div(i, bit), 2)
 
 
-def gather_kernel(faces, tiles, we_ref, ns_ref, we_all, ns_all, tsend, trecv, nsend, nrecv, fsend, frecv, gsend, grecv):
+def gather_kernel(faces, tiles, summed, *refs):
+    refs = list(refs)
+    we_ref, ns_ref = refs[:2]
+    sum_ref = refs[2] if summed else None
+    refs = refs[2 + summed :]
+    we_all, ns_all = refs[:2]
+    total = refs[2] if summed else None
+    refs = refs[2 + summed :]
+    wsend, wrecv, nsend, nrecv, fsend, frecv = refs[:6]
+    landed, ssend, srecv = refs[6:] if summed else (None, None, None)
     face = lax.axis_index("face")
     tile = lax.axis_index("tile")
-    tile_bits = [1 << b for b in range(tiles.bit_length() - 1)]
+    tile_bits = [1 << b for b in reversed(range(tiles.bit_length() - 1))]
     face_bits = [1 << b for b in reversed(range(faces.bit_length() - 1))]
     barrier = pltpu.get_barrier_semaphore()
     for bit in tile_bits:
@@ -232,6 +241,8 @@
     for bit in face_bits:
         pl.semaphore_signal(barrier, inc=1, device_id=(flipped_bit(face, bit), tile), device_id_type=MESH_ID)
     we_all[face, tile] = we_ref[...]
+    if summed:
+        total[...] = sum_ref[...]
 
     @pl.when(tile == 0)
     def _():
@@ -242,86 +253,148 @@
         ns_all[face, 1] = ns_ref[1]
 
     pl.semaphore_wait(barrier, len(tile_bits) + len(face_bits))
+
+    def share_sum(i, partner):
+        if not summed:
+            return None
+        copy = pltpu.make_async_remote_copy(
+            total, landed.at[i], ssend.at[i], srecv.at[i], partner, MESH_ID
+        )
+        copy.start()
+        return copy
+
+    def take_sum(i, copy):
+        if summed:
+            copy.wait()
+            total[...] = total[...] + landed[i]
+
+    held = [tile]
+    slot = 0
     for i, bit in enumerate(tile_bits):
         partner = (face, flipped_bit(tile, bit))
-        block = we_all.at[face, pl.ds(lax.div(tile, bit) * bit, bit)]
-        copy = pltpu.make_async_remote_copy(block, block, tsend.at[i], trecv.at[i], partner, MESH_ID)
-        copy.start()
+        copies = []
+        for h in held:
+            block = we_all.at[face, h]
+            copies.append(pltpu.make_async_remote_copy(block, block, wsend.at[slot], wrecv.at[slot], partner, MESH_ID))
+            slot += 1
+        for copy in copies:
+            copy.start()
         lines = []
         for side, place in enumerate((tile, tiles - 1 - tile)):
             line = ns_all.at[face, side]
             send = pltpu.make_async_remote_copy(
                 line, line, nsend.at[side, i], nrecv.at[side, i], partner, MESH_ID
             )
+            place = lax.rem(place, 2 * bit)
             lines.append((place, send))
 
-            @pl.when(place < bit)
+            @pl.when(place == 0)
             def _():
                 send.start()
 
-        copy.wait()
+        summing = share_sum(i, partner)
+        for copy in copies:
+            copy.wait()
         for place, send in lines:
 
-            @pl.when(place < bit)
+            @pl.when(place == 0)
             def _():
                 send.wait_send()
 
-            @pl.when((place >= bit) & (place < 2 * bit))
+            @pl.when(place == bit)
             def _():
                 send.wait_recv()
 
+        take_sum(i, summing)
+        held = held + [flipped_bit(h, bit) for h in held]
+
     held = [face]
     slot = 0
-    for bit in face_bits:
+    for i, bit in enumerate(face_bits):
         partner = (flipped_bit(face, bit), tile)
         copies = []
         for h in held:
-            block = we_all.at[h]
-            copies.append(pltpu.make_async_remote_copy(block, block, fsend.at[slot], frecv.at[slot], partner, MESH_ID))
-            lines = ns_all.at[h]
-            copies.append(pltpu.make_async_remote_copy(lines, lines, gsend.at[slot], grecv.at[slot], partner, MESH_ID))
-            slot += 1
+            for part in (we_all.at[h], ns_all.at[h]):
+                copies.append(pltpu.make_async_remote_copy(part, part, fsend.at[slot], frecv.at[slot], partner, MESH_ID))
+                slot += 1
         for copy in copies:
             copy.start()
+        summing = share_sum(len(tile_bits) + i, partner)
         for copy in copies:
             copy.wait()
+        take_sum(len(tile_bits) + i, summing)
         held = held + [flipped_bit(h, bit) for h in held]
 
 
-def gather_lines(we, ns):
+def gather_lines(we, ns, addend):
     faces, tiles = lax.axis_size("face"), lax.axis_size("tile")
     steps = tiles.bit_length() - 1
+    every = steps + faces.bit_length() - 1
     dma = pltpu.SemaphoreType.DMA
+    summed = addend is not None
+    operands = [we, ns]
+    outs = [
+        jax.ShapeDtypeStruct((faces, tiles) + we.shape, BF16),
+        jax.ShapeDtypeStruct((faces,) + ns.shape, BF16),
+    ]
+    scratch = [
+        dma((tiles,)), dma((tiles,)), dma((2, steps)), dma((2, steps)), dma((2 * faces,)), dma((2 * faces,)),
+    ]
+    if summed:
+        operands.append(addend)
+        outs.append(jax.ShapeDtypeStruct(addend.shape, F32))
+        scratch += [pltpu.VMEM((every,) + addend.shape, F32), dma((every,)), dma((every,))]
     return pl.pallas_call(
-        functools.partial(gather_kernel, faces, tiles),
-        in_specs=[pl.BlockSpec(memory_space=pltpu.VMEM)] * 2,
-        out_specs=[pl.BlockSpec(memory_space=pltpu.VMEM)] * 2,
-        out_shape=[
-            jax.ShapeDtypeStruct((faces, tiles) + we.shape, BF16),
-            jax.ShapeDtypeStruct((faces,) + ns.shape, BF16),
-        ],
-        scratch_shapes=[
-            dma((steps,)), dma((steps,)), dma((2, steps)), dma((2, steps)),
-            dma((faces,)), dma((faces,)), dma((faces,)), dma((faces,)),
-        ],
-        compiler_params=pltpu.CompilerParams(collective_id=0, has_side_effects=True),
-    )(we, ns)
-
-
-def exchange(north, south, west, east, links):
+        functools.partial(gather_kernel, faces, tiles, summed),
+        in_specs=[pl.BlockSpec(memory_space=pltpu.VMEM)] * len(operands),
+        out_specs=[pl.BlockSpec(memory_space=pltpu.VMEM)] * len(outs),
+        out_shape=outs,
+        scratch_shapes=scratch,
+        compiler_params=pltpu.CompilerParams(collective_id=int(summed), has_side_effects=True),
+    )(*operands)
+
+
+def pick_kernel(links_ref, we_ref, ns_ref, out_ref):
+    tiles, channels, side = we_ref.shape[1:]
+    faces_dev = ns_ref.shape[2]
+    seg = side // tiles
+    lane = lax.broadcasted_iota(jnp.int32, (channels, side), 1)
+    column = lax.broadcasted_iota(jnp.int32, (side, side), 1)
+    row = lax.broadcasted_iota(jnp.int32, (side, side), 0)
+    mirror = (row + column == side - 1).astype(F32).astype(BF16)
+
+    def pick(j, carry):
+        face, edge, flip = links_ref[3 * j], links_ref[3 * j + 1], links_ref[3 * j + 2]
+        group, local = lax.div(face, faces_dev), lax.rem(face, faces_dev)
+        straight = ns_ref[group, jnp.minimum(edge, 1), local].astype(F32)
+        offset = (local * 2 + jnp.maximum(edge - 2, 0)) * seg
+        across = jnp.zeros((channels, side), F32)
+        for t in range(tiles):
+            moved = pltpu.roll(we_ref[group, t].astype(F32), lax.rem(t * seg - offset + side, side), 1)
+            across = jnp.where((lane >= t * seg) & (lane < (t + 1) * seg), moved, across)
+        line = jnp.where(edge < 2, straight, across)
+        turned = jnp.dot(line.astype(BF16), mirror, preferred_element_type=F32)
+        out_ref[j] = jnp.where(flip == 1, turned, line).astype(BF16)
+        return carry
+
+    lax.fori_loop(0, out_ref.shape[0], pick, 0)
+
+
+def exchange(north, south, west, east, links, addend=None):
     faces_dev, channels, side = north.shape
     seg = west.shape[2]
-    we = jnp.stack([west, east], axis=1)
-    we = jnp.transpose(we, (2, 0, 1, 3)).reshape(channels, faces_dev * 2 * seg)
-    we_all, ns_all = gather_lines(we, jnp.stack([north, south]))
-    groups, tiles = we_all.shape[:2]
-    we_all = we_all.reshape(groups, tiles, channels, faces_dev, 2, seg)
-    we_all = jnp.transpose(we_all, (0, 3, 4, 2, 1, 5)).reshape(groups, faces_dev, 2, channels, side)
-    ns_all = jnp.transpose(ns_all, (0, 2, 1, 3, 4))
-    lines = jnp.concatenate([ns_all, we_all], axis=2).reshape(groups * faces_dev * 4, channels, side)
-    index = (links[:, :, 0] * 4 + links[:, :, 1]).reshape(-1)
-    picked = jnp.take(lines, index, axis=0, mode="clip").reshape(faces_dev, 4, channels, side)
-    return jnp.where((links[:, :, 2] == 1)[:, :, None, None], picked[..., ::-1], picked)
+    we = jnp.concatenate([e[f] for f in range(faces_dev) for e in (west, east)], axis=1)
+    we = jnp.pad(we, ((0, 0), (0, side - 2 * faces_dev * seg)))
+    gathered = gather_lines(we, jnp.stack([north, south]), addend)
+    vmem = pl.BlockSpec(memory_space=pltpu.VMEM)
+    ghosts = pl.pallas_call(
+        pick_kernel,
+        in_specs=[pl.BlockSpec(memory_space=pltpu.SMEM), vmem, vmem],
+        out_specs=vmem,
+        out_shape=jax.ShapeDtypeStruct((faces_dev * 4, channels, side), BF16),
+    )(links.reshape(-1), gathered[0], gathered[1])
+    ghosts = ghosts.reshape(faces_dev, 4, channels, side)
+    return ghosts, (gathered[2] if addend is not None else None)
 
 
 def halo(first, last):
@@ -334,7 +407,7 @@
 def fill(north, south, west, east, links, corners, pos, count):
     seg = west.shape[2]
     above, below = halo(north, south)
-    ghosts = exchange(north, south, west, east, links)
+    ghosts, _ = exchange(north, south, west, east, links)
     code = (corners == 0)[:, :, None]
     gn, gs, gw, ge = (ghosts[:, i] for i in range(4))
     nw = jnp.where(code[:, 0], gn[:, :, 0], gw[:, :, 0])
@@ -359,7 +432,7 @@
     return jnp.einsum("kc,fkq->fcq", flat, stacked, preferred_element_type=F32)
 
 
-def unfold_edges(north, south, west, east, weight, links, corners, pos, count):
+def unfold_edges(north, south, west, east, weight, links, corners, pos, count, addend):
     seg = west.shape[2]
     above, below = halo(north, south)
     rows = jnp.stack([above, below], axis=1)
@@ -381,15 +454,16 @@
     gs_line = gs[:, :, 1:-1] + ends(keep(2, sw), keep(3, se), side)
     gw_line = gw + ends(give(0, nw, at_top), give(2, sw, at_bottom), seg)
     ge_line = ge + ends(give(1, ne, at_top), give(3, se, at_bottom), seg)
-    ghosts = exchange(
-        gn_line.astype(BF16), gs_line.astype(BF16), gw_line.astype(BF16), ge_line.astype(BF16), links
-    ).astype(F32)
+    ghosts, total = exchange(
+        gn_line.astype(BF16), gs_line.astype(BF16), gw_line.astype(BF16), ge_line.astype(BF16), links, addend
+    )
+    ghosts = ghosts.astype(F32)
     columns = lax.dynamic_slice_in_dim(ghosts[:, 2:], pos * seg, seg, 3)
     columns = jnp.pad(columns, ((0, 0), (0, 0), (0, 0), (0, LANES - seg)))
     edges = jnp.stack(
         [jnp.where(at_top, ghosts[:, 0], zero), jnp.where(at_bottom, ghosts[:, 1], zero)], axis=1
     )
-    return rows, columns, edges
+    return rows, columns, edges, total
 
 
 def body(field_in, out_grad, weight_first, bias_first, weight_second, bias_second, face_links, corner_rules):
@@ -421,37 +495,38 @@
     def sides(edge):
         return edge[:, 0, :, :rows].astype(BF16), edge[:, 1, :, :rows].astype(BF16)
 
+    depth = 9 * channels
+
+    def packed(gw, gb):
+        both = jnp.concatenate([gw.T, jnp.sum(gb, axis=1, keepdims=True)], axis=1)
+        return jnp.pad(both, ((0, 0), (0, -both.shape[1] % LANES)))
+
     hhalo, hghost = fill(hidden[:, 0], hidden[:, -1], *sides(hedge), links, corners, pos, count)
     output, g2, gedge, gw2, gb2 = run_faces(
         second_kernel, [hidden, hhalo, hghost, og], [ahead(weight_second), bias_second[:, None]],
         [(full, BF16), (full, BF16), edge_out], sums, 1, 2 * flops,
     )
-    ghalo, gcol, grow = unfold_edges(
-        g2[:, 0], g2[:, -1], *sides(gedge), weight_second, links, corners, pos, count
+    ghalo, gcol, grow, sum2 = unfold_edges(
+        g2[:, 0], g2[:, -1], *sides(gedge), weight_second, links, corners, pos, count, packed(gw2, gb2)
     )
     g1, fedge, gw1, gb1 = run_faces(
         third_kernel, [g2, ghalo, gcol, grow, slope, x, xhalo, xghost], [behind(weight_second)],
         [(full, BF16), edge_out], sums, 2, 2 * flops,
     )
-    fhalo, fcol, frow = unfold_edges(
-        g1[:, 0], g1[:, -1], *sides(fedge), weight_first, links, corners, pos, count
+    fhalo, fcol, frow, sum1 = unfold_edges(
+        g1[:, 0], g1[:, -1], *sides(fedge), weight_first, links, corners, pos, count, packed(gw1, gb1)
     )
     (grad_field,) = run_faces(
         fourth_kernel, [g1, fhalo, fcol, frow], [behind(weight_first)], [(full, BF16)], [], 1, flops
     )
-    packed = jnp.concatenate(
-        [gw1, gw2, jnp.sum(gb1, axis=1)[None], jnp.sum(gb2, axis=1)[None]], axis=0
-    )
-    packed = lax.psum(packed, ("face", "tile")) / side
-    depth = 9 * channels
-    shaped = lambda g: jnp.transpose(g.reshape(3, 3, channels, channels), (3, 2, 0, 1))
+    shaped = lambda g: jnp.transpose(g[:, :depth].reshape(channels, 3, 3, channels), (0, 3, 1, 2)) / side
     return (
         swap(output),
         swap(grad_field),
-        shaped(packed[:depth]),
-        packed[2 * depth],
-        shaped(packed[depth : 2 * depth]),
-        packed[2 * depth + 1],
+        shaped(sum1),
+        sum1[:, depth] / side,
+        shaped(sum2),
+        sum2[:, depth] / side,
     )
 
 

time: 433 us -> 335 us (0.77)
  waiting for transfers between devices: 72.6 us -> 7.8 us
  local copies, waits for them, and re-layouts: 103 us -> 56.7 us
  Pallas kernels: 200 us -> 232 us
  between operations: 15.5 us -> 1.81 us
    psum x1 -> x0, waiting for transfers between devices: 65.3 us -> none  [body(): packed = lax.psum(packed, ('face', 'tile')) / side]
    pallas_call x4 -> x8, Pallas kernels: 117 us -> 149 us  [the longest x4 128 us: gather_lines(): pl.pallas_call(functools.partial(gather_kernel, faces, tiles, summed), in...]
    reshape x15 -> x1, local copies, waits for them, and re-layouts: 30.3 us -> 0.62 us  [exchange(): links.reshape(-1)]
    pallas_call x4 -> x0, local copies, waits for them, and re-layouts: 10.2 us -> none  [gather_lines(): pl.pallas_call(functools.partial(gather_kernel, faces, tiles), in_specs=[...]
    gather x4 -> x0, local copies, waits for them, and re-layouts: 6.08 us -> none  [exchange(): jnp.take(lines, index, axis=0, mode='clip')]
    unnamed x118 -> x92, local copies, waits for them, and re-layouts: 33.9 us -> 34.1 us
  transfers between devices with their start and end apart: 9 -> 8, of which waited for: 4 -> 3; matrix products, arithmetic and copies ran while one was open for 15% -> 12% of each run, Pallas kernels for 17% -> 10%
where the time goes in v2:
time: 335 us; the launch traced here: 334 us
  Pallas kernels  232 us (69%)
  local copies, waits for them, and re-layouts  56.7 us (17%)
  starting transfers between devices  18.6 us (6%)
  other arithmetic  15.5 us (5%)
  waiting for transfers between devices  7.8 us (2%)
    pallas_call x4, Pallas kernels, gather_lines(): pl.pallas_call(functools.partial(gather_kernel, faces, tiles, summed), in...  128 us
    pallas_call x4, Pallas kernels, run_faces(): pl.pallas_call(kernel, grid=(faces,), in_specs=[per_face(a.shape) for a i...  82.9 us
    unnamed x92, local copies, waits for them, and re-layouts  34.1 us
    pallas_call x4, Pallas kernels, exchange(): pl.pallas_call(pick_kernel, in_specs=[pl.BlockSpec(memory_space=pltpu.SME...  20.7 us
    ppermute x8, starting transfers between devices, halo(): return (lax.ppermute(last, 'tile', down), lax.ppermute(first, 'tile', up))  18.6 us
    ppermute x8, waiting for transfers between devices, halo(): return (lax.ppermute(last, 'tile', down), lax.ppermute(first, 'tile', up))  7.8 us
  transfers between devices with their start and end apart: 8, of which 3 were waited for; matrix products, arithmetic and copies ran while one was open for 12% of the time, Pallas kernels for 10%

profile of v2, /device:TPU:0, one launch (start us, length us, event | category | flops | bytes accessed | tf_op | source)
XLA Modules:
  0.0 334.0 jit_solution(2759350583062051967)
XLA Ops:
  0.6 1.5 fusion.63
  2.8 5.5 %collective-permute-start = (bf16[3,48,256]{2,1,0:T(8,128)(2,1)}, bf16[3,48,256]{2,1,0:T(8,128)(2,1)}, u32[]{:S(2)}, u32[]{:S(2)}) collective-permute-start(bf16[3,48,256]{2,1,0:T(8,128)(2,1)} %bitcast.256), channel_id=1, source_target_pairs={{0,1},{1,2},{2,3},{3,4},{4,5},{5,6},{6,7},{8,9},{9,10},{10,11},{11... | collective-permute-start | bytes 221192 | tf_op jit(solution)/shard_map/ppermute | solution.py:404
  8.9 1.4 collective-permute-start.1
  10.3 3.1 fusion.64
  22.1 2.0 copy.159
  27.6 1.6 pad_maximum_fusion.2.refs_1_
  29.2 27.9 %shard_map.127 = (bf16[4,8,48,256]{3,2,1,0:T(8,128)(2,1)}, bf16[4,2,3,48,256]{4,3,2,1,0:T(8,128)(2,1)}) custom-call(bf16[48,256]{1,0:T(8,128)(2,1)} %pad.116.refs_0_, bf16[2,3,48,256]{3,2,1,0:T(8,128)(2,1)} %pad_maximum_fusion.2.refs_1_), custom_call_target="tpu_custom_call" | custom-call | tf_op jit(solution)/shard_map/pallas_call | solution.py:347
  57.1 5.1 %shard_map.128 = bf16[12,48,256]{2,1,0:T(8,128)(2,1)} custom-call(s32[36]{0:T(128)} %reshape.174.links_ref, bf16[4,8,48,256]{3,2,1,0:T(8,128)(2,1)} %get-tuple-element.28.we_ref, bf16[4,2,3,48,256]{4,3,2,1,0:T(8,128)(2,1)} %get-tuple-element.29.ns_ref), custom_call_target="tpu_custom_call" | custom-call | tf_op jit(solution)/shard_map/pallas_call | solution.py:390
  64.5 4.5 %copy.184 = bf16[3,48,32,256]{3,1,2,0:T(8,128)(2,1)} copy(bf16[3,48,32,256]{3,2,1,0:T(8,128)(2,1)} %param.9) | data formatting | bytes 4718592 | tf_op args[1]
  71.4 14.8 %shard_map.129 = (bf16[3,32,48,256]{3,2,1,0:T(8,128)(2,1)S(1)}, f32[3,32,48,256]{3,2,1,0:T(8,128)S(1)}, f32[3,2,48,128]{3,2,1,0:T(8,128)S(1)}) custom-call(bf16[3,32,48,256]{3,2,1,0:T(8,128)(2,1)S(1)} %bitcast.258, bf16[3,2,48,256]{3,2,1,0:T(8,128)(2,1)S(1)} %copy.85.halo_ref.xhalo_ref, f32[3,2,48,128]{3,2,1,0:T(8,128)S(1)} %pad_convert_fusion.1.ghost_ref.xghost_ref, ...), custom_call_target="tpu_custom_call" | custom-call | flops 1019215872 | bytes 10000000 | tf_op jit(solution)/shard_map/pallas_call | solution.py:208
  86.2 2.1 copy-done.1
  88.4 1.4 copy-done.9
  91.2 25.2 %shard_map.130 = (bf16[4,8,48,256]{3,2,1,0:T(8,128)(2,1)}, bf16[4,2,3,48,256]{4,3,2,1,0:T(8,128)(2,1)}) custom-call(bf16[48,256]{1,0:T(8,128)(2,1)} %pad.119.refs_0_, bf16[2,3,48,256]{3,2,1,0:T(8,128)(2,1)} %pad_maximum_fusion.4.refs_1_), custom_call_target="tpu_custom_call" | custom-call | tf_op jit(solution)/shard_map/pallas_call | solution.py:347
  116.4 5.2 %shard_map.131 = bf16[12,48,256]{2,1,0:T(8,128)(2,1)} custom-call(s32[36]{0:T(128)} %reshape.174.links_ref, bf16[4,8,48,256]{3,2,1,0:T(8,128)(2,1)} %get-tuple-element.32.we_ref, bf16[4,2,3,48,256]{4,3,2,1,0:T(8,128)(2,1)} %get-tuple-element.33.ns_ref), custom_call_target="tpu_custom_call" | custom-call | tf_op jit(solution)/shard_map/pallas_call | solution.py:390
  122.7 1.8 collective-permute-start.2
  126.5 4.2 %collective-permute-done.3 = bf16[3,48,256]{2,1,0:T(8,128)(2,1)S(1)} collective-permute-done((bf16[3,48,256]{2,1,0:T(8,128)(2,1)S(1)}, bf16[3,48,256]{2,1,0:T(8,128)(2,1)S(1)}, u32[]{:S(2)}, u32[]{:S(2)}) %collective-permute-start.3) | collective-permute-done | bytes 73760 | tf_op jit(solution)/shard_map/ppermute | solution.py:404
  131.7 1.7 copy-done.10
  133.4 26.2 %shard_map.132 = (bf16[3,32,48,256]{3,2,1,0:T(8,128)(2,1)S(1)}, bf16[3,32,48,256]{3,2,1,0:T(8,128)(2,1)S(1)}, f32[3,2,48,128]{3,2,1,0:T(8,128)S(1)}, f32[432,48]{1,0:T(8,128)S(1)}, f32[48,256]{1,0:T(8,128)S(1)}) custom-call(bf16[3,32,48,256]{3,2,1,0:T(8,128)(2,1)S(1)} %copy-done.10, bf16[3,2,48,256]{3,2,1,0:T(8,128)(2,1)S(1)} %copy.95.halo_ref, ...), custom_call_target="tpu_custom_call" | custom-call | flops 2038431744 | bytes 10000000 | tf_op jit(solution)/shard_map/pallas_call | solution.py:208
  159.6 1.4 copy-done.8
  161.0 1.4 copy-done.3
  163.2 4.6 %collective-permute-start.4 = (bf16[3,48,256]{2,1,0:T(8,128)(2,1)S(1)}, bf16[3,48,256]{2,1,0:T(8,128)(2,1)}, u32[]{:S(2)}, u32[]{:S(2)}) collective-permute-start(bf16[3,48,256]{2,1,0:T(8,128)(2,1)S(1)} %get-tuple-element.78), channel_id=1, source_target_pairs={{0,1},{1,2},{2,3},{3,4},{4,5},{5,6},{6,7},{8,9},{9,10},{10,11},{11... | collective-permute-start | bytes 221192 | tf_op jit(solution)/shard_map/ppermute | solution.py:404
  170.4 4.1 %copy.126 = bf16[3,48,32,256]{3,2,1,0:T(8,128)(2,1)} copy(bf16[3,48,32,256]{3,1,2,0:T(8,128)(2,1)} %bitcast.262) | data formatting | bytes 4718592
  180.5 35.2 %shard_map.133 = (bf16[4,8,48,256]{3,2,1,0:T(8,128)(2,1)}, bf16[4,2,3,48,256]{4,3,2,1,0:T(8,128)(2,1)}, f32[48,512]{1,0:T(8,128)}) custom-call(bf16[48,256]{1,0:T(8,128)(2,1)} %pad.130.refs_0_, bf16[2,3,48,256]{3,2,1,0:T(8,128)(2,1)} %pad_maximum_fusion.7.refs_1_, f32[48,512]{1,0:T(8,128)} %select_maximum_fusion.1.refs_2_), custom_call_target="tpu_custom_call" | custom-call | tf_op jit(solution)/shard_map/pallas_call | solution.py:347
  215.8 5.1 %shard_map.134 = bf16[12,48,256]{2,1,0:T(8,128)(2,1)} custom-call(s32[36]{0:T(128)} %reshape.174.links_ref, bf16[4,8,48,256]{3,2,1,0:T(8,128)(2,1)} %get-tuple-element.39.we_ref, bf16[4,2,3,48,256]{4,3,2,1,0:T(8,128)(2,1)} %get-tuple-element.40.ns_ref), custom_call_target="tpu_custom_call" | custom-call | tf_op jit(solution)/shard_map/pallas_call | solution.py:390
  224.2 2.3 copy-done.2
  226.5 30.2 %shard_map.135 = (bf16[3,32,48,256]{3,2,1,0:T(8,128)(2,1)S(1)}, f32[3,2,48,128]{3,2,1,0:T(8,128)S(1)}, f32[432,48]{1,0:T(8,128)S(1)}, f32[48,256]{1,0:T(8,128)S(1)}) custom-call(bf16[3,32,48,256]{3,2,1,0:T(8,128)(2,1)S(1)} %copy-done.4, bf16[3,2,48,256]{3,2,1,0:T(8,128)(2,1)S(1)} %pad_maximum_fusion.6.halo_ref, f32[3,2,48,128]{3,2,1,0:T(8,128)S(1)} %pad.136.col_ref, ...), custom_call_target="tpu_custom_call" | custom-call | flops 2038431744 | bytes 10000000 | tf_op jit(solution)/shard_map/pallas_call | solution.py:208
  258.3 1.5 collective-permute-start.6
  265.6 3.4 %collective-permute-done.7 = bf16[3,48,256]{2,1,0:T(8,128)(2,1)S(1)} collective-permute-done((bf16[3,48,256]{2,1,0:T(8,128)(2,1)S(1)}, bf16[3,48,256]{2,1,0:T(8,128)(2,1)S(1)}, u32[]{:S(2)}, u32[]{:S(2)}) %collective-permute-start.7) | collective-permute-done | bytes 73760 | tf_op jit(solution)/shard_map/ppermute | solution.py:404
  270.9 40.1 %shard_map.136 = (bf16[4,8,48,256]{3,2,1,0:T(8,128)(2,1)}, bf16[4,2,3,48,256]{4,3,2,1,0:T(8,128)(2,1)}, f32[48,512]{1,0:T(8,128)}) custom-call(bf16[48,256]{1,0:T(8,128)(2,1)} %pad.145.refs_0_, bf16[2,3,48,256]{3,2,1,0:T(8,128)(2,1)} %pad_maximum_fusion.9.refs_1_, f32[48,512]{1,0:T(8,128)} %select_maximum_fusion.refs_2_), custom_call_target="tpu_custom_call" | custom-call | tf_op jit(solution)/shard_map/pallas_call | solution.py:347
  311.0 5.3 %shard_map.137 = bf16[12,48,256]{2,1,0:T(8,128)(2,1)} custom-call(s32[36]{0:T(128)} %reshape.174.links_ref, bf16[4,8,48,256]{3,2,1,0:T(8,128)(2,1)} %get-tuple-element.46.we_ref, bf16[4,2,3,48,256]{4,3,2,1,0:T(8,128)(2,1)} %get-tuple-element.47.ns_ref), custom_call_target="tpu_custom_call" | custom-call | tf_op jit(solution)/shard_map/pallas_call | solution.py:390
  319.2 11.7 %shard_map.138 = bf16[3,32,48,256]{3,2,1,0:T(8,128)(2,1)S(1)} custom-call(bf16[3,32,48,256]{3,2,1,0:T(8,128)(2,1)S(1)} %copy-done.6, bf16[3,2,48,256]{3,2,1,0:T(8,128)(2,1)S(1)} %pad_maximum_fusion.8.halo_ref, f32[3,2,48,128]{3,2,1,0:T(8,128)S(1)} %pad.151.col_ref, f32[3,2,48,256]{3,2,1,0:T(8,128)S(1)} %pad_maximum_fusion.1.row_ref, ...), custom_call_target="tpu_custom_call" | custom-call | flops 1019215872 | bytes 10000000 | tf_op jit(solution)/shard_map/pallas_call | solution.py:208
  330.9 2.2 copy.127
  (219 shorter events, 48.7 us)
Async XLA Ops:
  0.6 24.8 %copy-start = (s32[12,4,3]{0,1,2:T(4,128)S(1)}, s32[12,4,3]{0,1,2:T(4,128)}, u32[]{:S(2)}) copy-start(s32[12,4,3]{0,1,2:T(4,128)} %param.14) | copy-start | bytes 1732
  2.8 67.6 %collective-permute-start = (bf16[3,48,256]{2,1,0:T(8,128)(2,1)}, bf16[3,48,256]{2,1,0:T(8,128)(2,1)}, u32[]{:S(2)}, u32[]{:S(2)}) collective-permute-start(bf16[3,48,256]{2,1,0:T(8,128)(2,1)} %bitcast.256), channel_id=1, source_target_pairs={{0,1},{1,2},{2,3},{3,4},{4,5},{5,6},{6,7},{8,9},{9,10},{10,11},{11... | collective-permute-start | bytes 221192 | tf_op jit(solution)/shard_map/ppermute | solution.py:404
  8.9 4.5 %copy-start.11 = (bf16[3,48,32,256]{3,2,1,0:T(8,128)(2,1)S(1)}, bf16[3,48,32,256]{3,2,1,0:T(8,128)(2,1)}, u32[]{:S(2)}) copy-start(bf16[3,48,32,256]{3,2,1,0:T(8,128)(2,1)} %param.8) | copy-start | bytes 7077892
  8.9 61.5 %collective-permute-start.1 = (bf16[3,48,256]{2,1,0:T(8,128)(2,1)}, bf16[3,48,256]{2,1,0:T(8,128)(2,1)}, u32[]{:S(2)}, u32[]{:S(2)}) collective-permute-start(bf16[3,48,256]{2,1,0:T(8,128)(2,1)} %bitcast.218.clone.2), channel_id=1, source_target_pairs={{1,0},{2,1},{3,2},{4,3},{5,4},{6,5},{7,6},{9,8},{10,9},{11,10},{12... | collective-permute-start | bytes 221192 | tf_op jit(solution)/shard_map/ppermute | solution.py:404
  20.7 42.6 %copy-start.36 = (s32[12,4]{0,1:T(4,128)S(1)}, s32[12,4]{0,1:T(4,128)}, u32[]{:S(2)}) copy-start(s32[12,4]{0,1:T(4,128)} %param.15) | copy-start | bytes 580
  27.6 36.7 %copy-start.37 = (f32[48]{0:T(128)S(1)}, f32[48]{0:T(128)}, u32[]{:S(2)}) copy-start(f32[48]{0:T(128)} %param.11) | copy-start | bytes 580
  64.5 4.7 %copy-start.38 = (f32[48]{0:T(128)S(1)}, f32[48]{0:T(128)}, u32[]{:S(2)}) copy-start(f32[48]{0:T(128)} %param.13) | copy-start | bytes 580
  64.5 5.0 %copy-start.15 = (bf16[48,48,3,3]{1,0,3,2:T(8,128)(2,1)S(1)}, bf16[48,48,3,3]{1,0,3,2:T(8,128)(2,1)}, u32[]{:S(2)}) copy-start(bf16[48,48,3,3]{1,0,3,2:T(8,128)(2,1)} %rev.7) | copy-start | bytes 124420
  64.5 6.0 %copy-start.12 = (bf16[12,48,256]{2,1,0:T(8,128)(2,1)S(1)}, bf16[12,48,256]{2,1,0:T(8,128)(2,1)}, u32[]{:S(2)}) copy-start(bf16[12,48,256]{2,1,0:T(8,128)(2,1)} %shard_map.128) | copy-start | bytes 884740
  121.5 10.2 %copy-start.7 = (bf16[3,48,32,256]{3,1,2,0:T(8,128)(2,1)S(1)}, bf16[3,48,32,256]{3,1,2,0:T(8,128)(2,1)}, u32[]{:S(2)}) copy-start(bf16[3,48,32,256]{3,1,2,0:T(8,128)(2,1)} %copy.184) | copy-start | bytes 7077892
  122.7 3.8 %collective-permute-start.2 = (bf16[3,48,256]{2,1,0:T(8,128)(2,1)S(1)}, bf16[3,48,256]{2,1,0:T(8,128)(2,1)S(1)}, u32[]{:S(2)}, u32[]{:S(2)}) collective-permute-start(bf16[3,48,256]{2,1,0:T(8,128)(2,1)S(1)} %get-tuple-element.80), channel_id=1, source_target_pairs={{0,1},{1,2},{2,3},{3,4},{4,5},{5,6},{6,7},{8,9},{9,10},{10,11},{11... | collective-permute-start | bytes 221192 | tf_op jit(solution)/shard_map/ppermute | solution.py:404
  124.5 6.2 %collective-permute-start.3 = (bf16[3,48,256]{2,1,0:T(8,128)(2,1)S(1)}, bf16[3,48,256]{2,1,0:T(8,128)(2,1)S(1)}, u32[]{:S(2)}, u32[]{:S(2)}) collective-permute-start(bf16[3,48,256]{2,1,0:T(8,128)(2,1)S(1)} %get-tuple-element.81), channel_id=1, source_target_pairs={{1,0},{2,1},{3,2},{4,3},{5,4},{6,5},{7,6},{9,8},{10,9},{11,10},{12... | collective-permute-start | bytes 221192 | tf_op jit(solution)/shard_map/ppermute | solution.py:404
  163.2 13.8 %collective-permute-start.4 = (bf16[3,48,256]{2,1,0:T(8,128)(2,1)S(1)}, bf16[3,48,256]{2,1,0:T(8,128)(2,1)}, u32[]{:S(2)}, u32[]{:S(2)}) collective-permute-start(bf16[3,48,256]{2,1,0:T(8,128)(2,1)S(1)} %get-tuple-element.78), channel_id=1, source_target_pairs={{0,1},{1,2},{2,3},{3,4},{4,5},{5,6},{6,7},{8,9},{9,10},{10,11},{11... | collective-permute-start | bytes 221192 | tf_op jit(solution)/shard_map/ppermute | solution.py:404
  168.6 9.2 %collective-permute-start.5 = (bf16[3,48,256]{2,1,0:T(8,128)(2,1)S(1)}, bf16[3,48,256]{2,1,0:T(8,128)(2,1)}, u32[]{:S(2)}, u32[]{:S(2)}) collective-permute-start(bf16[3,48,256]{2,1,0:T(8,128)(2,1)S(1)} %get-tuple-element.79), channel_id=1, source_target_pairs={{1,0},{2,1},{3,2},{4,3},{5,4},{6,5},{7,6},{9,8},{10,9},{11,10},{12... | collective-permute-start | bytes 221192 | tf_op jit(solution)/shard_map/ppermute | solution.py:404
  170.3 4.5 %copy-start.32 = (pred[3]{0:T(512)(128)(4,1)S(1)}, pred[3]{0:T(512)(128)(4,1)}, u32[]{:S(2)}) copy-start(pred[3]{0:T(512)(128)(4,1)} %get-tuple-element.62) | copy-start | bytes 13
  170.3 4.5 %copy-start.33 = (pred[3]{0:T(512)(128)(4,1)S(1)}, pred[3]{0:T(512)(128)(4,1)}, u32[]{:S(2)}) copy-start(pred[3]{0:T(512)(128)(4,1)} %get-tuple-element.64) | copy-start | bytes 13
  170.3 4.5 %copy-start.34 = (pred[3]{0:T(512)(128)(4,1)S(1)}, pred[3]{0:T(512)(128)(4,1)}, u32[]{:S(2)}) copy-start(pred[3]{0:T(512)(128)(4,1)} %get-tuple-element.67) | copy-start | bytes 13
  170.4 4.5 %copy-start.35 = (pred[3]{0:T(512)(128)(4,1)S(1)}, pred[3]{0:T(512)(128)(4,1)}, u32[]{:S(2)}) copy-start(pred[3]{0:T(512)(128)(4,1)} %get-tuple-element.69) | copy-start | bytes 13
  170.4 4.7 %copy-start.18 = (bf16[3,48,258]{2,1,0:T(8,128)(2,1)S(1)}, bf16[3,48,258]{2,1,0:T(8,128)(2,1)}, u32[]{:S(2)}) copy-start(bf16[3,48,258]{2,1,0:T(8,128)(2,1)} %get-tuple-element.157) | copy-start | bytes 222916
  170.4 4.7 %copy-start.19 = (bf16[3,48,258]{2,1,0:T(8,128)(2,1)S(1)}, bf16[3,48,258]{2,1,0:T(8,128)(2,1)}, u32[]{:S(2)}) copy-start(bf16[3,48,258]{2,1,0:T(8,128)(2,1)} %get-tuple-element.158) | copy-start | bytes 222916
  170.4 4.7 %copy-start.20 = (bf16[3,48,258]{2,1,0:T(8,128)(2,1)S(1)}, bf16[3,48,258]{2,1,0:T(8,128)(2,1)}, u32[]{:S(2)}) copy-start(bf16[3,48,258]{2,1,0:T(8,128)(2,1)} %get-tuple-element.159) | copy-start | bytes 222916
  170.4 4.7 %copy-start.30 = (bf16[48,48,1,3]{1,0,3,2:T(8,128)(2,1)S(1)}, bf16[48,48,1,3]{1,0,3,2:T(8,128)(2,1)}, u32[]{:S(2)}) copy-start(bf16[48,48,1,3]{1,0,3,2:T(8,128)(2,1)} %get-tuple-element.135) | copy-start | bytes 41476
  174.8 4.7 %copy-start.28 = (bf16[48,48,3,1]{1,0,3,2:T(8,128)(2,1)S(1)}, bf16[48,48,3,1]{1,0,3,2:T(8,128)(2,1)}, u32[]{:S(2)}) copy-start(bf16[48,48,3,1]{1,0,3,2:T(8,128)(2,1)} %get-tuple-element.133) | copy-start | bytes 41476
  226.5 35.0 %copy-start.27 = (bf16[48,48,1,3]{1,0,3,2:T(8,128)(2,1)S(1)}, bf16[48,48,1,3]{1,0,3,2:T(8,128)(2,1)}, u32[]{:S(2)}) copy-start(bf16[48,48,1,3]{1,0,3,2:T(8,128)(2,1)} %get-tuple-element.130) | copy-start | bytes 41476
  256.7 5.2 %copy-start.26 = (bf16[48,48,1,3]{1,0,3,2:T(8,128)(2,1)S(1)}, bf16[48,48,1,3]{1,0,3,2:T(8,128)(2,1)}, u32[]{:S(2)}) copy-start(bf16[48,48,1,3]{1,0,3,2:T(8,128)(2,1)} %get-tuple-element.131) | copy-start | bytes 41476
  256.7 5.6 %copy-start.16 = (f32[48,512]{1,0:T(8,128)S(1)}, f32[48,512]{1,0:T(8,128)}, u32[]{:S(2)}) copy-start(f32[48,512]{1,0:T(8,128)} %get-tuple-element.49) | copy-start | bytes 294916
  258.3 7.3 %collective-permute-start.6 = (bf16[3,48,256]{2,1,0:T(8,128)(2,1)S(1)}, bf16[3,48,256]{2,1,0:T(8,128)(2,1)S(1)}, u32[]{:S(2)}, u32[]{:S(2)}) collective-permute-start(bf16[3,48,256]{2,1,0:T(8,128)(2,1)S(1)} %get-tuple-element.76), channel_id=1, source_target_pairs={{0,1},{1,2},{2,3},{3,4},{4,5},{5,6},{6,7},{8,9},{9,10},{10,11},{11... | collective-permute-start | bytes 221192 | tf_op jit(solution)/shard_map/ppermute | solution.py:404
  259.9 9.1 %collective-permute-start.7 = (bf16[3,48,256]{2,1,0:T(8,128)(2,1)S(1)}, bf16[3,48,256]{2,1,0:T(8,128)(2,1)S(1)}, u32[]{:S(2)}, u32[]{:S(2)}) collective-permute-start(bf16[3,48,256]{2,1,0:T(8,128)(2,1)S(1)} %get-tuple-element.77), channel_id=1, source_target_pairs={{1,0},{2,1},{3,2},{4,3},{5,4},{6,5},{7,6},{9,8},{10,9},{11,10},{12... | collective-permute-start | bytes 221192 | tf_op jit(solution)/shard_map/ppermute | solution.py:404
  261.9 7.4 %copy-start.25 = (bf16[48,48,3,1]{1,0,3,2:T(8,128)(2,1)S(1)}, bf16[48,48,3,1]{1,0,3,2:T(8,128)(2,1)}, u32[]{:S(2)}) copy-start(bf16[48,48,3,1]{1,0,3,2:T(8,128)(2,1)} %get-tuple-element.128) | copy-start | bytes 41476
  262.3 7.6 %copy-start.24 = (bf16[48,48,3,1]{1,0,3,2:T(8,128)(2,1)S(1)}, bf16[48,48,3,1]{1,0,3,2:T(8,128)(2,1)}, u32[]{:S(2)}) copy-start(bf16[48,48,3,1]{1,0,3,2:T(8,128)(2,1)} %get-tuple-element.129) | copy-start | bytes 41476
  310.9 7.3 %copy-start.17 = (f32[48,512]{1,0:T(8,128)S(1)}, f32[48,512]{1,0:T(8,128)}, u32[]{:S(2)}) copy-start(f32[48,512]{1,0:T(8,128)} %get-tuple-element.48) | copy-start | bytes 294916
  311.0 8.2 %copy-start.6 = (bf16[3,32,48,256]{3,2,1,0:T(8,128)(2,1)S(1)}, bf16[3,32,48,256]{3,2,1,0:T(8,128)(2,1)}, u32[]{:S(2)}) copy-start(bf16[3,32,48,256]{3,2,1,0:T(8,128)(2,1)} %copy-done.5) | copy-start | bytes 7077892
  (15 other events, 40.5 us)
